TPU v7x, 128 devices: a whole 4x4x4 slice. The times are simulated.
128 devices in a mesh: heads: 8 (over z, core), keys: 16 (over x, y).
Axes of the slice: x: 4, y: 4, z: 4, core: 2. Of those that a mesh axis runs over, the one named last changes fastest.
Arguments:
- queries: bfloat16 [4096, 4096], P('keys', 'heads')
- key_states: bfloat16 [131072, 4096], P('keys', 'heads')
- value_states: bfloat16 [131072, 4096], P('keys', 'heads'), may hold values from -6 to 6
- block_ids: int32 [32, 3072], P('heads', 'keys'), may hold values from 0 to 2047, as said below
- block_counts: int32 [32, 16], P('heads', 'keys'), may hold values from 2 to 192, as said below
- out_weight: bfloat16 [4096, 4096], P('heads'), may hold values from -0.09375 to 0.09375
Outputs:
- projected: bfloat16 [4096, 4096], P('keys', 'heads')
Inputs may be any that keep to these rules, and one draw needn't show every extreme that they name: `block_ids`: entry h, r * 192 + j names query block b // 64 and tile b % 64 of key range r for head h; the first block_counts[h, r] entries of a head and key range are distinct, the rest are ignored; every query block is named by a counted entry of every head. `block_counts`: some head and key range has exactly 192 counted entries.
All inputs are finite; a program needn't handle non-finite values.
Results may differ from a plain program's by a relative error of at most 0.025.
Values may be sent and summed in bfloat16 or wider, within the bound.
No kernel may reach another device: no remote copies, remote signals or barrier semaphores. Data moves between devices by JAX's collectives and lax.ppermute only.
A program may use at most 192 MiB of HBM per device.

v0:
```python
import functools
import math

import jax
import jax.numpy as jnp
from jax import lax
from jax.experimental import pallas as pl
from jax.experimental.pallas import tpu as pltpu
from jax.sharding import PartitionSpec as P

BLOCK = 128
UNROLL = 16
STAT_ROWS = 16
ABSENT = -3.0e38
Z_STEPS = (1, 3, 2)
F32 = jnp.float32
BF16 = jnp.bfloat16


def split3(x):
    high = x.astype(BF16).astype(F32)
    rest = x - high
    middle = rest.astype(BF16).astype(F32)
    return high, middle, rest - middle


def plan_kernel(tiles, owned, ids, counts, entries, starts):
    heads = ids.shape[0]
    zero = jnp.int32(0)

    def over_head(h, at):
        for c in range(owned):
            starts[c, h] = at[c]

        def one(j, at):
            block = ids[h, j]
            query = lax.div(block, jnp.int32(tiles))
            tile = lax.rem(block, jnp.int32(tiles))
            chunk = lax.rem(query, jnp.int32(owned))
            owner = lax.div(query, jnp.int32(owned))
            place = at[0]
            for c in range(1, owned):
                place = jnp.where(chunk == c, at[c], place)
            entries[chunk, place] = (h * 256 + owner) * 256 + tile
            return tuple(a + jnp.where(chunk == c, 1, 0) for c, a in enumerate(at))

        return lax.fori_loop(0, counts[h, 0], one, at)

    at = lax.fori_loop(0, heads, over_head, (zero,) * owned)
    for c in range(owned):
        starts[c, heads] = at[c]


def plan(ids, counts, tiles, owned):
    heads, slots = ids.shape
    smem = pl.BlockSpec(memory_space=pltpu.SMEM)
    return pl.pallas_call(
        functools.partial(plan_kernel, tiles, owned),
        out_shape=(
            jax.ShapeDtypeStruct((owned, heads * slots), jnp.int32),
            jax.ShapeDtypeStruct((owned, heads + 1), jnp.int32),
        ),
        in_specs=[smem, smem],
        out_specs=(smem, smem),
        name="plan",
    )(ids, counts)


def attend_kernel(
    chunk, entries, starts, q_hbm, k_hbm, v_hbm, out_ref, qs, ks, vs, acc, top, den, stats, sems
):
    heads, _, width = ks.shape
    owners = qs.shape[1] // BLOCK
    scale = width**-0.5 * math.log2(math.e)

    def copies(h):
        lanes = pl.ds(h * width, width)
        return [
            pltpu.make_async_copy(src.at[:, lanes], dst.at[h], sems.at[h, i])
            for i, (src, dst) in enumerate(((q_hbm, qs), (k_hbm, ks), (v_hbm, vs)))
        ]

    for h in range(heads):
        for copy in copies(h):
            copy.start()
    acc[...] = jnp.zeros_like(acc)
    den[...] = jnp.zeros_like(den)
    top[...] = jnp.full_like(top, -jnp.inf)
    count = starts[chunk, heads]
    groups = lax.div(count + UNROLL - 1, jnp.int32(UNROLL))
    opens = [lax.div(starts[chunk, h], jnp.int32(UNROLL)) for h in range(heads)]

    def group(step, carry):
        for h in range(heads):

            @pl.when(step == opens[h])
            def _():
                for copy in copies(h):
                    copy.wait()

        slots = []
        for u in range(UNROLL):
            j = step * UNROLL + u
            live = j < count
            entry = jnp.where(live, entries[chunk, j], 0)
            head = lax.shift_right_logical(entry, 16)
            owner = lax.bitwise_and(lax.shift_right_logical(entry, 8), 255)
            tile = lax.bitwise_and(entry, 255)
            slots.append((jnp.where(live, head * owners + owner, heads * owners), head, owner, tile))

        def rows(i):
            return pl.ds(pl.multiple_of(i * BLOCK, BLOCK), BLOCK)

        scores = [
            lax.dot_general(
                ks[head, rows(tile), :],
                qs[head, rows(owner), :],
                (((1,), (1,)), ((), ())),
                preferred_element_type=F32,
            )
            for _, head, owner, tile in slots
        ]
        parts = []
        for (slot, head, _, tile), s in zip(slots, scores):
            s = s * scale
            m = jnp.max(s, axis=0, keepdims=True)
            p = jnp.exp2(s - m)
            d = jnp.sum(p, axis=0, keepdims=True)
            o = lax.dot_general(
                vs[head, rows(tile), :],
                p.astype(BF16),
                (((0,), (0,)), ((), ())),
                preferred_element_type=F32,
            )
            parts.append((slot, m, d, o))
        for slot, m, d, o in parts:
            row = pl.ds(slot, 1)
            old = top[row, :]
            new = jnp.maximum(old, m)
            keep = jnp.exp2(old - new)
            take = jnp.exp2(m - new)
            top[row, :] = new
            den[row, :] = den[row, :] * keep + d * take
            acc[slot] = acc[slot] * keep + o * take
        return carry

    lax.fori_loop(0, groups, group, 0)
    for h in range(heads):

        @pl.when(opens[h] >= groups)
        def _():
            for copy in copies(h):
                copy.wait()

    used = heads * owners
    total = den[0:used, :]
    listed = total > 0
    safe = jnp.where(listed, total, 1.0)
    level = jnp.where(listed, top[0:used, :] + jnp.log2(safe), ABSENT)
    den[0:used, :] = jnp.where(listed, 1.0 / safe, 0.0)
    for h in range(heads):
        for q in range(owners):
            at = h * owners + q
            out_ref[q, h * width : (h + 1) * width, :] = (acc[at] * den[at : at + 1, :]).astype(BF16)
        for i, piece in enumerate(split3(level[h * owners : (h + 1) * owners])):
            stats[3 * h + i] = piece
    first = out_ref.shape[1] - STAT_ROWS
    for q in range(owners):
        rows = [stats[i, q : q + 1, :] for i in range(3 * heads)]
        rows.append(jnp.zeros((STAT_ROWS - 3 * heads, BLOCK), F32))
        out_ref[q, first:, :] = jnp.concatenate(rows, axis=0).astype(BF16)


def attend(chunk, entries, starts, queries, keys, values, heads):
    width = queries.shape[1] // heads
    owners = queries.shape[0] // BLOCK
    smem = pl.BlockSpec(memory_space=pltpu.SMEM)
    hbm = pl.BlockSpec(memory_space=pltpu.HBM)
    lines = -(-(heads * owners + 1) // 8) * 8
    return pl.pallas_call(
        functools.partial(attend_kernel, chunk),
        out_shape=jax.ShapeDtypeStruct((owners, heads * width + STAT_ROWS, BLOCK), BF16),
        in_specs=[smem, smem, hbm, hbm, hbm],
        scratch_shapes=[
            pltpu.VMEM((heads, queries.shape[0], width), BF16),
            pltpu.VMEM((heads, keys.shape[0], width), BF16),
            pltpu.VMEM((heads, values.shape[0], width), BF16),
            pltpu.VMEM((heads * owners + 1, width, BLOCK), F32),
            pltpu.VMEM((lines, BLOCK), F32),
            pltpu.VMEM((lines, BLOCK), F32),
            pltpu.VMEM((3 * heads, owners, BLOCK), F32),
            pltpu.SemaphoreType.DMA((heads, 3)),
        ],
        compiler_params=pltpu.CompilerParams(vmem_limit_bytes=48 * 1024 * 1024),
        name="attend",
    )(entries, starts, queries, keys, values)


def project_kernel(heads, core, in_ref, own_weight, other_weight, own_ref, other_ref, mixed):
    ranges, total, rows = in_ref.shape
    width = (total - STAT_ROWS) // heads
    first = total - STAT_ROWS

    @pl.when(pl.program_id(0) == 0)
    def _():
        stats = in_ref[:, first:, :].astype(F32)
        for h in range(heads):
            level = stats[:, 3 * h, :] + stats[:, 3 * h + 1, :] + stats[:, 3 * h + 2, :]
            share = jnp.exp2(level - jnp.max(level, axis=0, keepdims=True))
            share = share / jnp.sum(share, axis=0, keepdims=True)
            acc = jnp.zeros((width, rows), F32)
            for r in range(ranges):
                acc += in_ref[r, h * width : (h + 1) * width, :].astype(F32) * share[r : r + 1, :]
            mixed[h * width : (h + 1) * width, :] = acc.astype(BF16)

    for weight, out_ref in ((own_weight, own_ref), (other_weight, other_ref)):
        out_ref[0] = lax.dot_general(
            mixed[...], weight[...], (((0,), (0,)), ((), ())), preferred_element_type=F32
        ).astype(BF16)


def project(core, parts, weight, heads, span):
    depth = weight.shape[0]
    zs = weight.shape[1] // span // 2
    rows = parts.shape[2]
    result = pl.BlockSpec((1, rows, span), lambda z, core: (z, 0, 0))
    return pl.pallas_call(
        functools.partial(project_kernel, heads),
        out_shape=[jax.ShapeDtypeStruct((zs, rows, span), BF16)] * 2,
        grid_spec=pltpu.PrefetchScalarGridSpec(
            num_scalar_prefetch=1,
            grid=(zs,),
            in_specs=[
                pl.BlockSpec(parts.shape, lambda z, core: (0, 0, 0)),
                pl.BlockSpec((depth, span), lambda z, core: (0, 2 * z + core[0])),
                pl.BlockSpec((depth, span), lambda z, core: (0, 2 * z + 1 - core[0])),
            ],
            out_specs=[result, result],
            scratch_shapes=[pltpu.VMEM((depth, rows), BF16)],
        ),
        compiler_params=pltpu.CompilerParams(
            dimension_semantics=("arbitrary",), vmem_limit_bytes=32 * 1024 * 1024
        ),
        name="project",
    )(core, parts, weight, weight)


def pair_kernel(z, mine, theirs, own, *others):
    zs = mine.shape[0]
    for d, out in zip((0,) + Z_STEPS, (own,) + others):
        at = lax.rem(z[0] + d, jnp.int32(zs))
        out[...] = (mine[at].astype(F32) + theirs[at].astype(F32)).astype(out.dtype)


def pair(z, mine, theirs):
    shape = mine.shape[1:]
    vmem = pl.BlockSpec(memory_space=pltpu.VMEM)
    return pl.pallas_call(
        pair_kernel,
        out_shape=[jax.ShapeDtypeStruct(shape, F32)]
        + [jax.ShapeDtypeStruct(shape, BF16) for _ in Z_STEPS],
        in_specs=[pl.BlockSpec(memory_space=pltpu.SMEM), vmem, vmem],
        name="pair",
    )(z, mine, theirs)


def local(queries, key_states, value_states, block_ids, block_counts, out_weight):
    heads = block_ids.shape[0]
    ranges = lax.axis_size("keys")
    groups = lax.axis_size("heads")
    me = lax.axis_index("heads")
    core = jnp.reshape(me % 2, (1,)).astype(jnp.int32)
    z = jnp.reshape(me // 2, (1,)).astype(jnp.int32)
    span = out_weight.shape[1] // groups
    tiles = key_states.shape[0] // BLOCK
    owned = queries.shape[0] // BLOCK

    def exchange(parts):
        return lax.all_to_all(parts, "keys", split_axis=0, concat_axis=0, tiled=True)

    def finish(got):
        mine, theirs = project(core, got, out_weight, heads, span)
        swap = [(g, g ^ 1) for g in range(groups)]
        own, *others = pair(z, mine, lax.ppermute(theirs, "heads", swap))
        total = own
        for d, piece in zip(Z_STEPS, others):
            pairs = [(g, (g + 2 * d) % groups) for g in range(groups)]
            total = total + lax.ppermute(piece, "heads", pairs).astype(F32)
        return total.astype(BF16)

    def rows(c):
        return queries[c * BLOCK : (c + 1) * BLOCK]

    copies = jnp.broadcast_to(rows(0)[None], (ranges,) + rows(0).shape)
    first = exchange(copies).reshape(ranges * BLOCK, queries.shape[1])
    gathered = [first] + [
        lax.all_gather(rows(c), "keys", axis=0, tiled=True) for c in range(1, owned)
    ]
    entries, starts = plan(block_ids, block_counts, tiles, owned)
    outs = []
    for c in range(owned):
        parts = attend(c, entries, starts, gathered[c], key_states, value_states, heads)
        got = exchange(parts)
        if outs:
            got, outs[-1] = lax.optimization_barrier((got, outs[-1]))
        outs.append(finish(got))
    return jnp.concatenate(outs)


def solution(mesh):
    in_specs = (
        P("keys", "heads"),
        P("keys", "heads"),
        P("keys", "heads"),
        P("heads", "keys"),
        P("heads", "keys"),
        P("heads", None),
    )
    return jax.shard_map(
        local, mesh=mesh, in_specs=in_specs, out_specs=P("keys", "heads"), check_vma=False
    )
```

profile of v0, /device:TPU:0, one launch (start us, length us, event | category | flops | bytes accessed | tf_op | source)
XLA Modules:
  0.0 173.4 jit_solution(3182264116489895874)
XLA Ops:
  6.5 1.6 fusion
  9.7 7.2 %all-to-all-start.1 = ((bf16[16,128,512]{2,1,0:T(8,128)(2,1)}), bf16[16,128,512]{2,1,0:T(8,128)(2,1)S(1)}, u32[]{:S(2)}, u32[]{:S(2)}) async-start(bf16[16,128,512]{2,1,0:T(8,128)(2,1)} %broadcast_in_dim.2), calls=%async_computation.1 | async-start | bytes 4194304 | tf_op jit(solution)/shard_map/all_to_all | solution.py:279
  18.4 6.2 %plan.1 = (s32[2,768]{1,0:T(2,128)}, s32[2,5]{1,0:T(2,128)}) custom-call(s32[4,192]{1,0:T(4,128)} %ids.1, s32[4,1]{1,0:T(4,128)} %copy.7.counts), custom_call_target="tpu_custom_call" | custom-call | tf_op jit(solution)/shard_map/plan/pallas_call | solution.py:57
  24.6 23.2 %all-to-all-done.1 = bf16[16,128,512]{2,1,0:T(8,128)(2,1)S(1)} async-done(((bf16[16,128,512]{2,1,0:T(8,128)(2,1)}), bf16[16,128,512]{2,1,0:T(8,128)(2,1)S(1)}, u32[]{:S(2)}, u32[]{:S(2)}) %all-to-all-start.1) | async-done | bytes 2097184 | tf_op jit(solution)/shard_map/all_to_all | solution.py:279
  49.1 11.5 %attend.3 = bf16[16,528,128]{2,1,0:T(8,128)(2,1)} custom-call(s32[2,768]{1,0:T(2,128)S(1)} %copy-done.7, s32[2,5]{1,0:T(2,128)S(1)} %copy-done.9, bf16[2048,512]{1,0:T(8,128)(2,1)S(1)} %bitcast.3, bf16[8192,512]{1,0:T(8,128)(2,1)} %k_hbm.3, bf16[8192,512]{1,0:T(8,128)(2,1)} %v_hbm.3), custom_call_target="tpu_custom_call" | custom-call | tf_op jit(solution)/shard_map/attend/pallas_call | solution.py:180
  60.7 4.6 %all-to-all-start.2 = ((bf16[16,528,128]{2,1,0:T(8,128)(2,1)}), bf16[16,528,128]{2,1,0:T(8,128)(2,1)S(1)}, u32[]{:S(2)}, u32[]{:S(2)}) async-start(bf16[16,528,128]{2,1,0:T(8,128)(2,1)} %attend.3), calls=%async_computation.2 | async-start | bytes 4325376 | tf_op jit(solution)/shard_map/all_to_all | solution.py:279
  65.3 22.0 %all-gather.2.cloned.1.call-done.q_hbm = bf16[2048,512]{1,0:T(8,128)(2,1)} async-done(((bf16[128,512]{1,0:T(8,128)(2,1)}), bf16[2048,512]{1,0:T(8,128)(2,1)}) %all-gather.2.cloned.1.call-update) | async-done | bytes 2097168 | tf_op jit(solution)/shard_map/all_gather | solution.py:297
  88.9 11.1 %attend.2 = bf16[16,528,128]{2,1,0:T(8,128)(2,1)} custom-call(s32[2,768]{1,0:T(2,128)S(1)} %copy-done.8, s32[2,5]{1,0:T(2,128)S(1)} %copy-done.10, bf16[2048,512]{1,0:T(8,128)(2,1)S(1)} %copy-done.4, bf16[8192,512]{1,0:T(8,128)(2,1)} %k_hbm.3, bf16[8192,512]{1,0:T(8,128)(2,1)} %v_hbm.3), custom_call_target="tpu_custom_call" | custom-call | tf_op jit(solution)/shard_map/attend/pallas_call | solution.py:180
  101.3 11.9 %all-to-all-start = ((bf16[16,528,128]{2,1,0:T(8,128)(2,1)}), bf16[16,528,128]{2,1,0:T(8,128)(2,1)S(1)}, u32[]{:S(2)}, u32[]{:S(2)}) async-start(bf16[16,528,128]{2,1,0:T(8,128)(2,1)} %attend.2), calls=%async_computation | async-start | bytes 4325376 | tf_op jit(solution)/shard_map/all_to_all | solution.py:279
  113.2 2.2 %copy-done = bf16[512,4096]{1,0:T(8,128)(2,1)S(1)} copy-done((bf16[512,4096]{1,0:T(8,128)(2,1)S(1)}, bf16[512,4096]{1,0:T(8,128)(2,1)}, u32[]{:S(2)}) %copy-start) | copy-done | bytes 4194328
  117.0 2.3 %project.2 = (bf16[4,128,512]{2,1,0:T(8,128)(2,1)S(1)}, bf16[4,128,512]{2,1,0:T(8,128)(2,1)S(1)}) custom-call(s32[1]{0:T(128)} %bitcast.1.core, bf16[16,528,128]{2,1,0:T(8,128)(2,1)S(1)} %copy-done.3, bf16[512,4096]{1,0:T(8,128)(2,1)S(1)} %copy-done, bf16[512,4096]{1,0:T(8,128)(2,1)S(1)} %copy-done), custom_call_target="tpu_custom_call" | custom-call | tf_op jit(solution)/shard_map/project/pallas_call | solution.py:227
  120.1 1.9 %collective-permute-done.theirs = bf16[4,128,512]{2,1,0:T(8,128)(2,1)S(1)} collective-permute-done((bf16[4,128,512]{2,1,0:T(8,128)(2,1)S(1)}, bf16[4,128,512]{2,1,0:T(8,128)(2,1)S(1)}, u32[]{:S(2)}, u32[]{:S(2)}) %collective-permute-start) | collective-permute-done | bytes 524320 | tf_op jit(solution)/shard_map/ppermute | solution.py:284
  122.8 2.1 %pair.2 = (f32[128,512]{1,0:T(8,128)}, bf16[128,512]{1,0:T(8,128)(2,1)}, bf16[128,512]{1,0:T(8,128)(2,1)}, bf16[128,512]{1,0:T(8,128)(2,1)}) custom-call(s32[1]{0:T(128)} %bitcast.z, bf16[4,128,512]{2,1,0:T(8,128)(2,1)} %copy-done.5, bf16[4,128,512]{2,1,0:T(8,128)(2,1)} %copy-done.11), custom_call_target="tpu_custom_call" | custom-call | tf_op jit(solution)/shard_map/pair/pallas_call | solution.py:258
  124.9 2.6 %collective-permute-start.1 = (bf16[128,512]{1,0:T(8,128)(2,1)}, bf16[128,512]{1,0:T(8,128)(2,1)S(1)}, u32[]{:S(2)}, u32[]{:S(2)}) collective-permute-start(bf16[128,512]{1,0:T(8,128)(2,1)} %get-tuple-element.26), channel_id=1, source_target_pairs={{0,32},{16,48},{32,64},{48,80},{64,96},{80,112},{96,0},{112,16},{1... | collective-permute-start | bytes 393224 | tf_op jit(solution)/shard_map/ppermute | solution.py:288
  129.5 2.3 %collective-permute-done.1 = bf16[128,512]{1,0:T(8,128)(2,1)S(1)} collective-permute-done((bf16[128,512]{1,0:T(8,128)(2,1)}, bf16[128,512]{1,0:T(8,128)(2,1)S(1)}, u32[]{:S(2)}, u32[]{:S(2)}) %collective-permute-start.1) | collective-permute-done | bytes 131104 | tf_op jit(solution)/shard_map/ppermute | solution.py:288
  131.8 2.2 %collective-permute-done.2 = bf16[128,512]{1,0:T(8,128)(2,1)S(1)} collective-permute-done((bf16[128,512]{1,0:T(8,128)(2,1)}, bf16[128,512]{1,0:T(8,128)(2,1)S(1)}, u32[]{:S(2)}, u32[]{:S(2)}) %collective-permute-start.2) | collective-permute-done | bytes 131104 | tf_op jit(solution)/shard_map/ppermute | solution.py:288
  135.8 9.0 %all-to-all-done.in_ref = bf16[16,528,128]{2,1,0:T(8,128)(2,1)S(1)} async-done(((bf16[16,528,128]{2,1,0:T(8,128)(2,1)}), bf16[16,528,128]{2,1,0:T(8,128)(2,1)S(1)}, u32[]{:S(2)}, u32[]{:S(2)}) %all-to-all-start) | async-done | bytes 2162720 | tf_op jit(solution)/shard_map/all_to_all | solution.py:279
  144.8 2.2 %copy-done.1 = bf16[512,4096]{1,0:T(8,128)(2,1)S(1)} copy-done((bf16[512,4096]{1,0:T(8,128)(2,1)S(1)}, bf16[512,4096]{1,0:T(8,128)(2,1)}, u32[]{:S(2)}) %copy-start.1) | copy-done | bytes 4194328
  147.0 2.3 %project.3 = (bf16[4,128,512]{2,1,0:T(8,128)(2,1)S(1)}, bf16[4,128,512]{2,1,0:T(8,128)(2,1)S(1)}) custom-call(s32[1]{0:T(128)} %bitcast.1.core, bf16[16,528,128]{2,1,0:T(8,128)(2,1)S(1)} %all-to-all-done.in_ref, bf16[512,4096]{1,0:T(8,128)(2,1)S(1)} %copy-done.1, bf16[512,4096]{1,0:T(8,128)(2,1)S(1)} %copy-done.1), custom_call_target="tpu_custom_call" | custom-call | tf_op jit(solution)/shard_map/project/pallas_call | solution.py:227
  150.1 1.9 %collective-permute-done.4.theirs = bf16[4,128,512]{2,1,0:T(8,128)(2,1)S(1)} collective-permute-done((bf16[4,128,512]{2,1,0:T(8,128)(2,1)S(1)}, bf16[4,128,512]{2,1,0:T(8,128)(2,1)S(1)}, u32[]{:S(2)}, u32[]{:S(2)}) %collective-permute-start.4) | collective-permute-done | bytes 524320 | tf_op jit(solution)/shard_map/ppermute | solution.py:284
  152.8 2.1 %pair.3 = (f32[128,512]{1,0:T(8,128)}, bf16[128,512]{1,0:T(8,128)(2,1)}, bf16[128,512]{1,0:T(8,128)(2,1)}, bf16[128,512]{1,0:T(8,128)(2,1)}) custom-call(s32[1]{0:T(128)} %bitcast.z, bf16[4,128,512]{2,1,0:T(8,128)(2,1)} %copy-done.6, bf16[4,128,512]{2,1,0:T(8,128)(2,1)} %copy-done.12), custom_call_target="tpu_custom_call" | custom-call | tf_op jit(solution)/shard_map/pair/pallas_call | solution.py:258
  154.9 3.2 %collective-permute-start.6 = (bf16[128,512]{1,0:T(8,128)(2,1)}, bf16[128,512]{1,0:T(8,128)(2,1)S(1)}, u32[]{:S(2)}, u32[]{:S(2)}) collective-permute-start(bf16[128,512]{1,0:T(8,128)(2,1)} %get-tuple-element.35), channel_id=1, source_target_pairs={{0,96},{16,112},{32,0},{48,16},{64,32},{80,48},{96,64},{112,80},{1... | collective-permute-start | bytes 393224 | tf_op jit(solution)/shard_map/ppermute | solution.py:288
  158.1 3.7 %collective-permute-done.5 = bf16[128,512]{1,0:T(8,128)(2,1)S(1)} collective-permute-done((bf16[128,512]{1,0:T(8,128)(2,1)}, bf16[128,512]{1,0:T(8,128)(2,1)S(1)}, u32[]{:S(2)}, u32[]{:S(2)}) %collective-permute-start.5) | collective-permute-done | bytes 131104 | tf_op jit(solution)/shard_map/ppermute | solution.py:288
  161.9 2.2 %collective-permute-done.6 = bf16[128,512]{1,0:T(8,128)(2,1)S(1)} collective-permute-done((bf16[128,512]{1,0:T(8,128)(2,1)}, bf16[128,512]{1,0:T(8,128)(2,1)S(1)}, u32[]{:S(2)}, u32[]{:S(2)}) %collective-permute-start.6) | collective-permute-done | bytes 131104 | tf_op jit(solution)/shard_map/ppermute | solution.py:288
  (42 shorter events, 18.4 us)
Async XLA Ops:
  9.7 8.0 %copy-start.13 = (s32[4,1]{0,1:T(1,128)S(1)}, s32[4,1]{0,1:T(1,128)}, u32[]{:S(2)}) copy-start(s32[4,1]{0,1:T(1,128)} %param.10) | copy-start | bytes 52
  9.7 38.1 %all-to-all-start.1 = ((bf16[16,128,512]{2,1,0:T(8,128)(2,1)}), bf16[16,128,512]{2,1,0:T(8,128)(2,1)S(1)}, u32[]{:S(2)}, u32[]{:S(2)}) async-start(bf16[16,128,512]{2,1,0:T(8,128)(2,1)} %broadcast_in_dim.2), calls=%async_computation.1 | async-start | bytes 4194304 | tf_op jit(solution)/shard_map/all_to_all | solution.py:279
  17.0 70.3 %all-gather.2.cloned.1.call-start = ((), (), s32[]{:S(2)}) async-start(), calls=%async_computation.3 | async-start | bytes 2228224 | tf_op jit(solution)/shard_map/all_gather | solution.py:297
  60.7 26.6 %copy-start.8 = (s32[2,768]{1,0:T(2,128)S(1)}, s32[2,768]{1,0:T(2,128)}, u32[]{:S(2)}) copy-start(s32[2,768]{1,0:T(2,128)} %get-tuple-element.21.entries) | copy-start | bytes 18436
  60.7 26.6 %copy-start.10 = (s32[2,5]{1,0:T(2,128)S(1)}, s32[2,5]{1,0:T(2,128)}, u32[]{:S(2)}) copy-start(s32[2,5]{1,0:T(2,128)} %get-tuple-element.22.starts) | copy-start | bytes 124
  60.7 39.3 %all-to-all-start.2 = ((bf16[16,528,128]{2,1,0:T(8,128)(2,1)}), bf16[16,528,128]{2,1,0:T(8,128)(2,1)S(1)}, u32[]{:S(2)}, u32[]{:S(2)}) async-start(bf16[16,528,128]{2,1,0:T(8,128)(2,1)} %attend.3), calls=%async_computation.2 | async-start | bytes 4325376 | tf_op jit(solution)/shard_map/all_to_all | solution.py:279
  87.3 1.6 copy-start.4
  100.0 1.3 copy-start.2
  101.3 43.5 %all-to-all-start = ((bf16[16,528,128]{2,1,0:T(8,128)(2,1)}), bf16[16,528,128]{2,1,0:T(8,128)(2,1)S(1)}, u32[]{:S(2)}, u32[]{:S(2)}) async-start(bf16[16,528,128]{2,1,0:T(8,128)(2,1)} %attend.2), calls=%async_computation | async-start | bytes 4325376 | tf_op jit(solution)/shard_map/all_to_all | solution.py:279
  113.2 2.2 %copy-start = (bf16[512,4096]{1,0:T(8,128)(2,1)S(1)}, bf16[512,4096]{1,0:T(8,128)(2,1)}, u32[]{:S(2)}) copy-start(bf16[512,4096]{1,0:T(8,128)(2,1)} %other_weight.3) | copy-start | bytes 12582916
  115.4 1.6 copy-start.3
  119.3 0.8 copy-start.5
  120.1 1.9 %collective-permute-start = (bf16[4,128,512]{2,1,0:T(8,128)(2,1)S(1)}, bf16[4,128,512]{2,1,0:T(8,128)(2,1)S(1)}, u32[]{:S(2)}, u32[]{:S(2)}) collective-permute-start(bf16[4,128,512]{2,1,0:T(8,128)(2,1)S(1)} %get-tuple-element.24), channel_id=1, source_target_pairs={{0,16},{16,0},{32,48},{48,32},{64,80},{80,64},{96,112},{112,96},{1... | collective-permute-start | bytes 1572872 | tf_op jit(solution)/shard_map/ppermute | solution.py:284
  122.0 0.8 copy-start.11
  124.9 7.0 %collective-permute-start.1 = (bf16[128,512]{1,0:T(8,128)(2,1)}, bf16[128,512]{1,0:T(8,128)(2,1)S(1)}, u32[]{:S(2)}, u32[]{:S(2)}) collective-permute-start(bf16[128,512]{1,0:T(8,128)(2,1)} %get-tuple-element.26), channel_id=1, source_target_pairs={{0,32},{16,48},{32,64},{48,80},{64,96},{80,112},{96,0},{112,16},{1... | collective-permute-start | bytes 393224 | tf_op jit(solution)/shard_map/ppermute | solution.py:288
  127.4 6.6 %collective-permute-start.2 = (bf16[128,512]{1,0:T(8,128)(2,1)}, bf16[128,512]{1,0:T(8,128)(2,1)S(1)}, u32[]{:S(2)}, u32[]{:S(2)}) collective-permute-start(bf16[128,512]{1,0:T(8,128)(2,1)} %get-tuple-element.27), channel_id=1, source_target_pairs={{0,96},{16,112},{32,0},{48,16},{64,32},{80,48},{96,64},{112,80},{1... | collective-permute-start | bytes 393224 | tf_op jit(solution)/shard_map/ppermute | solution.py:288
  128.1 6.7 %collective-permute-start.3 = (bf16[128,512]{1,0:T(8,128)(2,1)}, bf16[128,512]{1,0:T(8,128)(2,1)S(1)}, u32[]{:S(2)}, u32[]{:S(2)}) collective-permute-start(bf16[128,512]{1,0:T(8,128)(2,1)} %get-tuple-element.28), channel_id=1, source_target_pairs={{0,64},{16,80},{32,96},{48,112},{64,0},{80,16},{96,32},{112,48},{1... | collective-permute-start | bytes 393224 | tf_op jit(solution)/shard_map/ppermute | solution.py:288
  144.8 2.2 %copy-start.1 = (bf16[512,4096]{1,0:T(8,128)(2,1)S(1)}, bf16[512,4096]{1,0:T(8,128)(2,1)}, u32[]{:S(2)}) copy-start(bf16[512,4096]{1,0:T(8,128)(2,1)} %other_weight.3) | copy-start | bytes 12582916
  149.3 0.8 copy-start.6
  150.1 1.9 %collective-permute-start.4 = (bf16[4,128,512]{2,1,0:T(8,128)(2,1)S(1)}, bf16[4,128,512]{2,1,0:T(8,128)(2,1)S(1)}, u32[]{:S(2)}, u32[]{:S(2)}) collective-permute-start(bf16[4,128,512]{2,1,0:T(8,128)(2,1)S(1)} %get-tuple-element.32), channel_id=1, source_target_pairs={{0,16},{16,0},{32,48},{48,32},{64,80},{80,64},{96,112},{112,96},{1... | collective-permute-start | bytes 1572872 | tf_op jit(solution)/shard_map/ppermute | solution.py:284
  152.0 0.8 copy-start.12
  154.9 7.0 %collective-permute-start.5 = (bf16[128,512]{1,0:T(8,128)(2,1)}, bf16[128,512]{1,0:T(8,128)(2,1)S(1)}, u32[]{:S(2)}, u32[]{:S(2)}) collective-permute-start(bf16[128,512]{1,0:T(8,128)(2,1)} %get-tuple-element.34), channel_id=1, source_target_pairs={{0,32},{16,48},{32,64},{48,80},{64,96},{80,112},{96,0},{112,16},{1... | collective-permute-start | bytes 393224 | tf_op jit(solution)/shard_map/ppermute | solution.py:288
  154.9 9.1 %collective-permute-start.6 = (bf16[128,512]{1,0:T(8,128)(2,1)}, bf16[128,512]{1,0:T(8,128)(2,1)S(1)}, u32[]{:S(2)}, u32[]{:S(2)}) collective-permute-start(bf16[128,512]{1,0:T(8,128)(2,1)} %get-tuple-element.35), channel_id=1, source_target_pairs={{0,96},{16,112},{32,0},{48,16},{64,32},{80,48},{96,64},{112,80},{1... | collective-permute-start | bytes 393224 | tf_op jit(solution)/shard_map/ppermute | solution.py:288
  158.1 6.7 %collective-permute-start.7 = (bf16[128,512]{1,0:T(8,128)(2,1)}, bf16[128,512]{1,0:T(8,128)(2,1)S(1)}, u32[]{:S(2)}, u32[]{:S(2)}) collective-permute-start(bf16[128,512]{1,0:T(8,128)(2,1)} %get-tuple-element.36), channel_id=1, source_target_pairs={{0,64},{16,80},{32,96},{48,112},{64,0},{80,16},{96,32},{112,48},{1... | collective-permute-start | bytes 393224 | tf_op jit(solution)/shard_map/ppermute | solution.py:288
  (2 other events, 1.3 us)
Sparse Core Ops, SparseCore 0:
  19.9 67.2 all-gather.1
where the time goes:
time: 173 us
  waiting for transfers between devices  70.7 us (41%)
  Pallas kernels  37.5 us (22%)
  starting transfers between devices  31.6 us (18%)
  local copies, waits for them, and re-layouts  17.3 us (10%)
  between operations  13.6 us (8%)
  other arithmetic  2.76 us (2%)
    all_to_all x3, waiting for transfers between devices, exchange(): lax.all_to_all(parts, 'keys', split_axis=0, concat_axis=0, tiled=True)  32.2 us
    all_to_all x3, starting transfers between devices, exchange(): lax.all_to_all(parts, 'keys', split_axis=0, concat_axis=0, tiled=True)  23.7 us
    pallas_call x2, Pallas kernels, attend(): pl.pallas_call(functools.partial(attend_kernel, chunk), out_shape=jax.Sha...  22.6 us
    all_gather x1, waiting for transfers between devices, local(): lax.all_gather(rows(c), 'keys', axis=0, tiled=True)  22 us
    unnamed x29, local copies, waits for them, and re-layouts  14.1 us
    ppermute x6, waiting for transfers between devices, finish(): total = total + lax.ppermute(piece, 'heads', pairs).astype(F32)  12 us
    ppermute x6, starting transfers between devices, finish(): total = total + lax.ppermute(piece, 'heads', pairs).astype(F32)  7.89 us
    pallas_call x1, Pallas kernels, plan(): pl.pallas_call(functools.partial(plan_kernel, tiles, owned), out_shape=(j...  6.2 us
  transfers between devices with their start and end apart: 12, of which 11 were waited for; matrix products, arithmetic and copies ran while one was open for 1% of the time, Pallas kernels for 19%

commit v1 on v0

--- a/solution.py
+++ b/solution.py
@@ -24,8 +24,10 @@
     return high, middle, rest - middle
 
 
-def plan_kernel(tiles, owned, ids, counts, entries, starts):
+def plan_kernel(tiles, owned, side, me, ids, counts, entries, starts):
     heads = ids.shape[0]
+    my_x = lax.div(me[0], jnp.int32(side))
+    my_y = lax.rem(me[0], jnp.int32(side))
     zero = jnp.int32(0)
 
     def over_head(h, at):
@@ -38,10 +40,14 @@
             tile = lax.rem(block, jnp.int32(tiles))
             chunk = lax.rem(query, jnp.int32(owned))
             owner = lax.div(query, jnp.int32(owned))
+            dx = lax.rem(my_x - lax.div(owner, jnp.int32(side)) + side, jnp.int32(side))
+            dy = lax.rem(my_y - lax.rem(owner, jnp.int32(side)) + side, jnp.int32(side))
+            near = jnp.where(h < heads // 2, dy * side + dx, dx * side + dy)
+            position = jnp.where(chunk == 0, near, owner)
             place = at[0]
             for c in range(1, owned):
                 place = jnp.where(chunk == c, at[c], place)
-            entries[chunk, place] = (h * 256 + owner) * 256 + tile
+            entries[chunk, place] = ((h * 256 + owner) * 256 + position) * 256 + tile
             return tuple(a + jnp.where(chunk == c, 1, 0) for c, a in enumerate(at))
 
         return lax.fori_loop(0, counts[h, 0], one, at)
@@ -51,33 +57,39 @@
         starts[c, heads] = at[c]
 
 
-def plan(ids, counts, tiles, owned):
+def plan(me, ids, counts, tiles, owned, side):
     heads, slots = ids.shape
     smem = pl.BlockSpec(memory_space=pltpu.SMEM)
     return pl.pallas_call(
-        functools.partial(plan_kernel, tiles, owned),
+        functools.partial(plan_kernel, tiles, owned, side),
         out_shape=(
             jax.ShapeDtypeStruct((owned, heads * slots), jnp.int32),
             jax.ShapeDtypeStruct((owned, heads + 1), jnp.int32),
         ),
-        in_specs=[smem, smem],
+        in_specs=[smem, smem, smem],
         out_specs=(smem, smem),
+        compiler_params=pltpu.CompilerParams(vmem_limit_bytes=1024 * 1024),
         name="plan",
-    )(ids, counts)
-
-
-def attend_kernel(
-    chunk, entries, starts, q_hbm, k_hbm, v_hbm, out_ref, qs, ks, vs, acc, top, den, stats, sems
-):
+    )(me, ids, counts)
+
+
+def attend_kernel(chunk, sources, entries, starts, *refs):
+    blocks = 1 + max(i for pieces in sources for i, _ in pieces)
+    q_hbm = refs[:blocks]
+    k_hbm, v_hbm, out_ref, qs, ks, vs, acc, top, den, stats, sems = refs[blocks:]
     heads, _, width = ks.shape
     owners = qs.shape[1] // BLOCK
     scale = width**-0.5 * math.log2(math.e)
 
     def copies(h):
-        lanes = pl.ds(h * width, width)
+        moves = [(k_hbm.at[:, h * width : (h + 1) * width], ks.at[h])]
+        moves.append((v_hbm.at[:, h * width : (h + 1) * width], vs.at[h]))
+        for n, (i, lane) in enumerate(sources[h]):
+            rows = q_hbm[i].shape[0]
+            src = q_hbm[i].at[:, lane * width : (lane + 1) * width]
+            moves.append((src, qs.at[h, n * rows : (n + 1) * rows]))
         return [
-            pltpu.make_async_copy(src.at[:, lanes], dst.at[h], sems.at[h, i])
-            for i, (src, dst) in enumerate(((q_hbm, qs), (k_hbm, ks), (v_hbm, vs)))
+            pltpu.make_async_copy(src, dst, sems.at[h, i]) for i, (src, dst) in enumerate(moves)
         ]
 
     for h in range(heads):
@@ -103,10 +115,12 @@
             j = step * UNROLL + u
             live = j < count
             entry = jnp.where(live, entries[chunk, j], 0)
-            head = lax.shift_right_logical(entry, 16)
-            owner = lax.bitwise_and(lax.shift_right_logical(entry, 8), 255)
+            head = lax.shift_right_logical(entry, 24)
+            owner = lax.bitwise_and(lax.shift_right_logical(entry, 16), 255)
+            position = lax.bitwise_and(lax.shift_right_logical(entry, 8), 255)
             tile = lax.bitwise_and(entry, 255)
-            slots.append((jnp.where(live, head * owners + owner, heads * owners), head, owner, tile))
+            slot = jnp.where(live, head * owners + owner, heads * owners)
+            slots.append((slot, head, position, tile))
 
         def rows(i):
             return pl.ds(pl.multiple_of(i * BLOCK, BLOCK), BLOCK)
@@ -114,11 +128,11 @@
         scores = [
             lax.dot_general(
                 ks[head, rows(tile), :],
-                qs[head, rows(owner), :],
+                qs[head, rows(position), :],
                 (((1,), (1,)), ((), ())),
                 preferred_element_type=F32,
             )
-            for _, head, owner, tile in slots
+            for _, head, position, tile in slots
         ]
         parts = []
         for (slot, head, _, tile), s in zip(slots, scores):
@@ -171,29 +185,35 @@
         out_ref[q, first:, :] = jnp.concatenate(rows, axis=0).astype(BF16)
 
 
-def attend(chunk, entries, starts, queries, keys, values, heads):
-    width = queries.shape[1] // heads
-    owners = queries.shape[0] // BLOCK
+def in_hbm(x):
+    return pltpu.with_memory_space_constraint(x, pltpu.HBM)
+
+
+def attend(chunk, entries, starts, queries, sources, keys, values):
+    heads = len(sources)
+    width = keys.shape[1] // heads
+    count = sum(queries[i].shape[0] for i, _ in sources[0])
+    owners = count // BLOCK
     smem = pl.BlockSpec(memory_space=pltpu.SMEM)
-    hbm = pl.BlockSpec(memory_space=pltpu.HBM)
+    hbm = pl.BlockSpec(memory_space=pl.ANY)
     lines = -(-(heads * owners + 1) // 8) * 8
     return pl.pallas_call(
-        functools.partial(attend_kernel, chunk),
+        functools.partial(attend_kernel, chunk, sources),
         out_shape=jax.ShapeDtypeStruct((owners, heads * width + STAT_ROWS, BLOCK), BF16),
-        in_specs=[smem, smem, hbm, hbm, hbm],
+        in_specs=[smem, smem] + [hbm] * (len(queries) + 2),
         scratch_shapes=[
-            pltpu.VMEM((heads, queries.shape[0], width), BF16),
+            pltpu.VMEM((heads, count, width), BF16),
             pltpu.VMEM((heads, keys.shape[0], width), BF16),
             pltpu.VMEM((heads, values.shape[0], width), BF16),
             pltpu.VMEM((heads * owners + 1, width, BLOCK), F32),
             pltpu.VMEM((lines, BLOCK), F32),
             pltpu.VMEM((lines, BLOCK), F32),
             pltpu.VMEM((3 * heads, owners, BLOCK), F32),
-            pltpu.SemaphoreType.DMA((heads, 3)),
+            pltpu.SemaphoreType.DMA((heads, 2 + max(len(p) for p in sources))),
         ],
         compiler_params=pltpu.CompilerParams(vmem_limit_bytes=48 * 1024 * 1024),
         name="attend",
-    )(entries, starts, queries, keys, values)
+    )(entries, starts, *queries, in_hbm(keys), in_hbm(values))
 
 
 def project_kernel(heads, core, in_ref, own_weight, other_weight, own_ref, other_ref, mixed):
@@ -242,7 +262,7 @@
             dimension_semantics=("arbitrary",), vmem_limit_bytes=32 * 1024 * 1024
         ),
         name="project",
-    )(core, parts, weight, weight)
+    )(core, parts, in_hbm(weight), in_hbm(weight))
 
 
 def pair_kernel(z, mine, theirs, own, *others):
@@ -254,12 +274,18 @@
 
 def pair(z, mine, theirs):
     shape = mine.shape[1:]
-    vmem = pl.BlockSpec(memory_space=pltpu.VMEM)
+    whole = pl.BlockSpec(mine.shape, lambda i, z: (0, 0, 0))
     return pl.pallas_call(
         pair_kernel,
         out_shape=[jax.ShapeDtypeStruct(shape, F32)]
         + [jax.ShapeDtypeStruct(shape, BF16) for _ in Z_STEPS],
-        in_specs=[pl.BlockSpec(memory_space=pltpu.SMEM), vmem, vmem],
+        grid_spec=pltpu.PrefetchScalarGridSpec(
+            num_scalar_prefetch=1,
+            grid=(1,),
+            in_specs=[whole, whole],
+            out_specs=[pl.BlockSpec(shape, lambda i, z: (0, 0))] * (1 + len(Z_STEPS)),
+        ),
+        compiler_params=pltpu.CompilerParams(vmem_limit_bytes=8 * 1024 * 1024),
         name="pair",
     )(z, mine, theirs)
 
@@ -274,6 +300,7 @@
     span = out_weight.shape[1] // groups
     tiles = key_states.shape[0] // BLOCK
     owned = queries.shape[0] // BLOCK
+    side = math.isqrt(ranges)
 
     def exchange(parts):
         return lax.all_to_all(parts, "keys", split_axis=0, concat_axis=0, tiled=True)
@@ -291,15 +318,37 @@
     def rows(c):
         return queries[c * BLOCK : (c + 1) * BLOCK]
 
-    copies = jnp.broadcast_to(rows(0)[None], (ranges,) + rows(0).shape)
-    first = exchange(copies).reshape(ranges * BLOCK, queries.shape[1])
-    gathered = [first] + [
-        lax.all_gather(rows(c), "keys", axis=0, tiled=True) for c in range(1, owned)
-    ]
-    entries, starts = plan(block_ids, block_counts, tiles, owned)
+    def along(x, axis):
+        def pairs(d):
+            there = lambda i, j: ((i + d) % side, j) if axis == 0 else (i, (j + d) % side)
+            moved = [there(k // side, k % side) for k in range(ranges)]
+            return [(k, i * side + j) for k, (i, j) in enumerate(moved)]
+
+        got = {d: lax.ppermute(x, "keys", pairs(d)) for d in Z_STEPS}
+        return [x] + [got[d] for d in range(1, side)]
+
+    near = rows(0)
+    middle = near.shape[1] // 2
+    left, right = near[:, :middle], near[:, middle:]
+    left, right = lax.optimization_barrier((left, right))
+    halves = along(left, 0) + along(right, 1)
+    halves = lax.optimization_barrier(halves)
+    left, right = jnp.concatenate(halves[:side]), jnp.concatenate(halves[side:])
+    left, right = lax.optimization_barrier((left, right))
+    direct = lax.optimization_barrier(along(left, 1) + along(right, 0))
+    lower = [[(i, h) for i in range(side)] for h in range(heads // 2)]
+    upper = [[(side + i, h) for i in range(side)] for h in range(heads // 2)]
+    whole = [[(0, h)] for h in range(heads)]
+
+    slot = jnp.reshape(lax.axis_index("keys"), (1,)).astype(jnp.int32)
+    entries, starts = plan(slot, block_ids, block_counts, tiles, owned, side)
     outs = []
     for c in range(owned):
-        parts = attend(c, entries, starts, gathered[c], key_states, value_states, heads)
+        if c == 0:
+            source, lanes = direct, lower + upper
+        else:
+            source, lanes = [in_hbm(lax.all_gather(rows(c), "keys", axis=0, tiled=True))], whole
+        parts = attend(c, entries, starts, source, lanes, key_states, value_states)
         got = exchange(parts)
         if outs:
             got, outs[-1] = lax.optimization_barrier((got, outs[-1]))

time: 173 us -> 157 us (0.908)
  waiting for transfers between devices: 70.7 us -> 40.1 us
  starting transfers between devices: 31.6 us -> 48.1 us
  Pallas kernels: 37.5 us -> 48 us
  local copies, waits for them, and re-layouts: 17.3 us -> 6.82 us
  other arithmetic: 2.76 us -> 0.88 us
    ppermute x0 -> x12, starting transfers between devices: none -> 22.4 us  [along(): got = {d: lax.ppermute(x, 'keys', pairs(d)) for d in Z_STEPS}]
    all_gather x1, waiting for transfers between devices: 22 us -> 0.02 us  [local(): lax.all_gather(rows(c), 'keys', axis=0, tiled=True)]
    all_to_all x3 -> x2, starting transfers between devices: 23.7 us -> 8.4 us  [exchange(): lax.all_to_all(parts, 'keys', split_axis=0, concat_axis=0, tiled=True)]
    all_to_all x3 -> x2, waiting for transfers between devices: 32.2 us -> 22.1 us  [exchange(): lax.all_to_all(parts, 'keys', split_axis=0, concat_axis=0, tiled=True)]
    pallas_call x3, Pallas kernels: 28.8 us -> 38.7 us  [the longest x2 26.8 us: attend(): pl.pallas_call(functools.partial(attend_kernel, chunk, sources), out_shap...]
    unnamed x29 -> x7, local copies, waits for them, and re-layouts: 14.1 us -> 4.37 us
    ppermute x6, starting transfers between devices: 7.89 us -> 17.2 us  [finish(): total = total + lax.ppermute(piece, 'heads', pairs).astype(F32)]
    ppermute x0 -> x12, waiting for transfers between devices: none -> 4.82 us  [along(): got = {d: lax.ppermute(x, 'keys', pairs(d)) for d in Z_STEPS}]
  transfers between devices with their start and end apart: 12 -> 23, of which waited for: 11 -> 12; matrix products, arithmetic and copies ran while one was open for 1% -> 1% of each run, Pallas kernels for 19% -> 28%
where the time goes in v1:
time: 157 us
  starting transfers between devices  48.1 us (31%)
  Pallas kernels  48 us (31%)
  waiting for transfers between devices  40.1 us (26%)
  between operations  13.6 us (9%)
  local copies, waits for them, and re-layouts  6.82 us (4%)
    pallas_call x2, Pallas kernels, attend(): pl.pallas_call(functools.partial(attend_kernel, chunk, sources), out_shap...  26.8 us
    ppermute x12, starting transfers between devices, along(): got = {d: lax.ppermute(x, 'keys', pairs(d)) for d in Z_STEPS}  22.4 us
    all_to_all x2, waiting for transfers between devices, exchange(): lax.all_to_all(parts, 'keys', split_axis=0, concat_axis=0, tiled=True)  22.1 us
    ppermute x6, starting transfers between devices, finish(): total = total + lax.ppermute(piece, 'heads', pairs).astype(F32)  17.2 us
    pallas_call x1, Pallas kernels, plan(): pl.pallas_call(functools.partial(plan_kernel, tiles, owned, side), out_sh...  11.8 us
    ppermute x6, waiting for transfers between devices, finish(): total = total + lax.ppermute(piece, 'heads', pairs).astype(F32)  9.16 us
    pallas_call x2, Pallas kernels, project(): pl.pallas_call(functools.partial(project_kernel, heads), out_shape=[jax.S...  9.09 us
    all_to_all x2, starting transfers between devices, exchange(): lax.all_to_all(parts, 'keys', split_axis=0, concat_axis=0, tiled=True)  8.4 us
  transfers between devices with their start and end apart: 23, of which 12 were waited for; matrix products, arithmetic and copies ran while one was open for 1% of the time, Pallas kernels for 28%

profile of v1, /device:TPU:0, one launch (start us, length us, event | category | flops | bytes accessed | tf_op | source)
XLA Modules:
  0.0 157.5 jit_solution(9163710613689194254)
XLA Ops:
  10.7 2.7 %collective-permute-start.1 = (bf16[128,256]{1,0:T(8,128)(2,1)S(1)}, bf16[128,256]{1,0:T(8,128)(2,1)S(1)}, u32[]{:S(2)}, u32[]{:S(2)}) collective-permute-start(bf16[128,256]{1,0:T(8,128)(2,1)S(1)} %get-tuple-element.45), channel_id=1, source_target_pairs={{0,8},{1,9},{2,10},{3,11},{4,12},{5,13},{6,14},{7,15},{8,0},{9,1},... | collective-permute-start | bytes 196616 | tf_op jit(solution)/shard_map/ppermute | solution.py:327
  16.4 2.9 %collective-permute-start.4 = (bf16[128,256]{1,0:T(8,128)(2,1)S(1)}, bf16[128,256]{1,0:T(8,128)(2,1)S(1)}, u32[]{:S(2)}, u32[]{:S(2)}) collective-permute-start(bf16[128,256]{1,0:T(8,128)(2,1)S(1)} %get-tuple-element.49), channel_id=1, source_target_pairs={{0,2},{1,3},{2,0},{3,1},{4,6},{5,7},{6,4},{7,5},{8,10},{9,11},{10,... | collective-permute-start | bytes 196616 | tf_op jit(solution)/shard_map/ppermute | solution.py:327
  24.2 2.8 %collective-permute-start.11 = (bf16[512,256]{1,0:T(8,128)(2,1)S(1)}, bf16[512,256]{1,0:T(8,128)(2,1)S(1)}, u32[]{:S(2)}, u32[]{:S(2)}) collective-permute-start(bf16[512,256]{1,0:T(8,128)(2,1)S(1)} %get-tuple-element.59.refs_4_), channel_id=1, source_target_pairs={{0,12},{1,13},{2,14},{3,15},{4,0},{5,1},{6,2},{7,3},{8,4},{9,5},{1... | collective-permute-start | bytes 786440 | tf_op jit(solution)/shard_map/ppermute | solution.py:327
  27.3 3.7 %collective-permute-start.7 = (bf16[512,256]{1,0:T(8,128)(2,1)S(1)}, bf16[512,256]{1,0:T(8,128)(2,1)S(1)}, u32[]{:S(2)}, u32[]{:S(2)}) collective-permute-start(bf16[512,256]{1,0:T(8,128)(2,1)S(1)} %get-tuple-element.55.refs_0_), channel_id=1, source_target_pairs={{0,2},{1,3},{2,0},{3,1},{4,6},{5,7},{6,4},{7,5},{8,10},{9,11},{10,... | collective-permute-start | bytes 786440 | tf_op jit(solution)/shard_map/ppermute | solution.py:327
  33.0 3.3 %collective-permute-start.9 = (bf16[512,256]{1,0:T(8,128)(2,1)S(1)}, bf16[512,256]{1,0:T(8,128)(2,1)S(1)}, u32[]{:S(2)}, u32[]{:S(2)}) collective-permute-start(bf16[512,256]{1,0:T(8,128)(2,1)S(1)} %get-tuple-element.59.refs_4_), channel_id=1, source_target_pairs={{0,4},{1,5},{2,6},{3,7},{4,8},{5,9},{6,10},{7,11},{8,12},{9,13},{1... | collective-permute-start | bytes 786440 | tf_op jit(solution)/shard_map/ppermute | solution.py:327
  37.7 11.8 %plan.1 = (s32[2,768]{1,0:T(2,128)S(1)}, s32[2,5]{1,0:T(2,128)S(1)}) custom-call(s32[1]{0:T(128)} %bitcast.me, s32[4,192]{1,0:T(4,128)S(1)} %copy-done.2, s32[4,1]{1,0:T(4,128)S(1)} %copy.7.counts), custom_call_target="tpu_custom_call" | custom-call | tf_op jit(solution)/shard_map/plan/pallas_call | solution.py:63
  49.6 13.9 %attend.3 = bf16[16,528,128]{2,1,0:T(8,128)(2,1)} custom-call(s32[2,768]{1,0:T(2,128)S(1)} %get-tuple-element.41.entries, s32[2,5]{1,0:T(2,128)S(1)} %get-tuple-element.42.starts, bf16[512,256]{1,0:T(8,128)(2,1)S(1)} %get-tuple-element.55.refs_0_, bf16[512,256]{1,0:T(8,128)(2,1)S(1)} %collective-permute-done.6.refs_1_, ...), custom_call_target="tpu_custom_call" | custom-call | tf_op jit(solution)/shard_map/attend/pallas_call | solution.py:200
  63.5 4.4 %all-to-all-start.1 = ((bf16[16,528,128]{2,1,0:T(8,128)(2,1)}), bf16[16,528,128]{2,1,0:T(8,128)(2,1)S(1)}, u32[]{:S(2)}, u32[]{:S(2)}) async-start(bf16[16,528,128]{2,1,0:T(8,128)(2,1)} %attend.3), calls=%async_computation.1 | async-start | bytes 4325376 | tf_op jit(solution)/shard_map/all_to_all | solution.py:306
  67.9 12.9 %attend.2 = bf16[16,528,128]{2,1,0:T(8,128)(2,1)} custom-call(s32[2,768]{1,0:T(2,128)S(1)} %get-tuple-element.41.entries, s32[2,5]{1,0:T(2,128)S(1)} %get-tuple-element.42.starts, bf16[2048,512]{1,0:T(8,128)(2,1)} %all-gather.2.cloned.1.call-done.refs_0_, bf16[8192,512]{1,0:T(8,128)(2,1)} %refs_8_.1, bf16[8192,512]{1,0:T(8,128)(2,1)} %refs_9_.1), custom_call_target="tpu_custom_call" | custom-call | tf_op jit(solution)/shard_map/attend/pallas_call | solution.py:200
  80.9 15.7 %all-to-all-done.1.in_ref = bf16[16,528,128]{2,1,0:T(8,128)(2,1)S(1)} async-done(((bf16[16,528,128]{2,1,0:T(8,128)(2,1)}), bf16[16,528,128]{2,1,0:T(8,128)(2,1)S(1)}, u32[]{:S(2)}, u32[]{:S(2)}) %all-to-all-start.1) | async-done | bytes 2162720 | tf_op jit(solution)/shard_map/all_to_all | solution.py:306
  97.9 4.0 %all-to-all-start = ((bf16[16,528,128]{2,1,0:T(8,128)(2,1)}), bf16[16,528,128]{2,1,0:T(8,128)(2,1)S(1)}, u32[]{:S(2)}, u32[]{:S(2)}) async-start(bf16[16,528,128]{2,1,0:T(8,128)(2,1)} %attend.2), calls=%async_computation | async-start | bytes 4325376 | tf_op jit(solution)/shard_map/all_to_all | solution.py:306
  103.6 5.0 %project.2 = (bf16[4,128,512]{2,1,0:T(8,128)(2,1)S(1)}, bf16[4,128,512]{2,1,0:T(8,128)(2,1)}) custom-call(s32[1]{0:T(128)} %bitcast.2.core, bf16[16,528,128]{2,1,0:T(8,128)(2,1)S(1)} %copy-done.1, bf16[512,4096]{1,0:T(8,128)(2,1)} %other_weight.3, bf16[512,4096]{1,0:T(8,128)(2,1)} %other_weight.3), custom_call_target="tpu_custom_call" | custom-call | tf_op jit(solution)/shard_map/project/pallas_call | solution.py:247
  108.6 2.1 %collective-permute-done.12.theirs = bf16[4,128,512]{2,1,0:T(8,128)(2,1)S(1)} collective-permute-done((bf16[4,128,512]{2,1,0:T(8,128)(2,1)}, bf16[4,128,512]{2,1,0:T(8,128)(2,1)S(1)}, u32[]{:S(2)}, u32[]{:S(2)}) %collective-permute-start.12) | collective-permute-done | bytes 524320 | tf_op jit(solution)/shard_map/ppermute | solution.py:311
  110.8 2.0 %collective-permute-start.13 = (bf16[128,512]{1,0:T(8,128)(2,1)S(1)}, bf16[128,512]{1,0:T(8,128)(2,1)S(1)}, u32[]{:S(2)}, u32[]{:S(2)}) collective-permute-start(bf16[128,512]{1,0:T(8,128)(2,1)S(1)} %get-tuple-element.66), channel_id=1, source_target_pairs={{0,32},{16,48},{32,64},{48,80},{64,96},{80,112},{96,0},{112,16},{1... | collective-permute-start | bytes 393224 | tf_op jit(solution)/shard_map/ppermute | solution.py:315
  114.1 5.4 %collective-permute-start.15 = (bf16[128,512]{1,0:T(8,128)(2,1)S(1)}, bf16[128,512]{1,0:T(8,128)(2,1)S(1)}, u32[]{:S(2)}, u32[]{:S(2)}) collective-permute-start(bf16[128,512]{1,0:T(8,128)(2,1)S(1)} %get-tuple-element.68), channel_id=1, source_target_pairs={{0,64},{16,80},{32,96},{48,112},{64,0},{80,16},{96,32},{112,48},{1... | collective-permute-start | bytes 393224 | tf_op jit(solution)/shard_map/ppermute | solution.py:315
  119.6 2.2 %collective-permute-done.14 = bf16[128,512]{1,0:T(8,128)(2,1)S(1)} collective-permute-done((bf16[128,512]{1,0:T(8,128)(2,1)S(1)}, bf16[128,512]{1,0:T(8,128)(2,1)S(1)}, u32[]{:S(2)}, u32[]{:S(2)}) %collective-permute-start.14) | collective-permute-done | bytes 131104 | tf_op jit(solution)/shard_map/ppermute | solution.py:315
  121.8 2.3 %collective-permute-done.15 = bf16[128,512]{1,0:T(8,128)(2,1)S(1)} collective-permute-done((bf16[128,512]{1,0:T(8,128)(2,1)S(1)}, bf16[128,512]{1,0:T(8,128)(2,1)S(1)}, u32[]{:S(2)}, u32[]{:S(2)}) %collective-permute-start.15) | collective-permute-done | bytes 131104 | tf_op jit(solution)/shard_map/ppermute | solution.py:315
  124.2 6.3 %all-to-all-done.in_ref = bf16[16,528,128]{2,1,0:T(8,128)(2,1)S(1)} async-done(((bf16[16,528,128]{2,1,0:T(8,128)(2,1)}), bf16[16,528,128]{2,1,0:T(8,128)(2,1)S(1)}, u32[]{:S(2)}, u32[]{:S(2)}) %all-to-all-start) | async-done | bytes 2162720 | tf_op jit(solution)/shard_map/all_to_all | solution.py:306
  130.5 4.1 %project.3 = (bf16[4,128,512]{2,1,0:T(8,128)(2,1)S(1)}, bf16[4,128,512]{2,1,0:T(8,128)(2,1)S(1)}) custom-call(s32[1]{0:T(128)} %bitcast.2.core, bf16[16,528,128]{2,1,0:T(8,128)(2,1)S(1)} %all-to-all-done.in_ref, bf16[512,4096]{1,0:T(8,128)(2,1)} %other_weight.3, bf16[512,4096]{1,0:T(8,128)(2,1)} %other_weight.3), custom_call_target="tpu_custom_call" | custom-call | tf_op jit(solution)/shard_map/project/pallas_call | solution.py:247
  134.7 1.9 %collective-permute-done.16.theirs = bf16[4,128,512]{2,1,0:T(8,128)(2,1)S(1)} collective-permute-done((bf16[4,128,512]{2,1,0:T(8,128)(2,1)S(1)}, bf16[4,128,512]{2,1,0:T(8,128)(2,1)S(1)}, u32[]{:S(2)}, u32[]{:S(2)}) %collective-permute-start.16) | collective-permute-done | bytes 524320 | tf_op jit(solution)/shard_map/ppermute | solution.py:311
  136.8 3.2 %collective-permute-start.18 = (bf16[128,512]{1,0:T(8,128)(2,1)S(1)}, bf16[128,512]{1,0:T(8,128)(2,1)S(1)}, u32[]{:S(2)}, u32[]{:S(2)}) collective-permute-start(bf16[128,512]{1,0:T(8,128)(2,1)S(1)} %get-tuple-element.75), channel_id=1, source_target_pairs={{0,96},{16,112},{32,0},{48,16},{64,32},{80,48},{96,64},{112,80},{1... | collective-permute-start | bytes 393224 | tf_op jit(solution)/shard_map/ppermute | solution.py:315
  140.1 5.2 %collective-permute-start.19 = (bf16[128,512]{1,0:T(8,128)(2,1)S(1)}, bf16[128,512]{1,0:T(8,128)(2,1)S(1)}, u32[]{:S(2)}, u32[]{:S(2)}) collective-permute-start(bf16[128,512]{1,0:T(8,128)(2,1)S(1)} %get-tuple-element.76), channel_id=1, source_target_pairs={{0,64},{16,80},{32,96},{48,112},{64,0},{80,16},{96,32},{112,48},{1... | collective-permute-start | bytes 393224 | tf_op jit(solution)/shard_map/ppermute | solution.py:315
  145.3 2.2 %collective-permute-done.18 = bf16[128,512]{1,0:T(8,128)(2,1)S(1)} collective-permute-done((bf16[128,512]{1,0:T(8,128)(2,1)S(1)}, bf16[128,512]{1,0:T(8,128)(2,1)S(1)}, u32[]{:S(2)}, u32[]{:S(2)}) %collective-permute-start.18) | collective-permute-done | bytes 131104 | tf_op jit(solution)/shard_map/ppermute | solution.py:315
  147.5 2.3 %collective-permute-done.19 = bf16[128,512]{1,0:T(8,128)(2,1)S(1)} collective-permute-done((bf16[128,512]{1,0:T(8,128)(2,1)S(1)}, bf16[128,512]{1,0:T(8,128)(2,1)S(1)}, u32[]{:S(2)}, u32[]{:S(2)}) %collective-permute-start.19) | collective-permute-done | bytes 131104 | tf_op jit(solution)/shard_map/ppermute | solution.py:315
  (43 shorter events, 21.3 us)
Async XLA Ops:
  6.5 61.4 %all-gather.2.cloned.1.call-start = ((), (), s32[]{:S(2)}) async-start(), calls=%async_computation.2 | async-start | bytes 2228224 | tf_op jit(solution)/shard_map/all_gather | solution.py:350
  9.0 10.3 %collective-permute-start = (bf16[128,256]{1,0:T(8,128)(2,1)S(1)}, bf16[128,256]{1,0:T(8,128)(2,1)S(1)}, u32[]{:S(2)}, u32[]{:S(2)}) collective-permute-start(bf16[128,256]{1,0:T(8,128)(2,1)S(1)} %get-tuple-element.45), channel_id=1, source_target_pairs={{0,4},{1,5},{2,6},{3,7},{4,8},{5,9},{6,10},{7,11},{8,12},{9,13},{1... | collective-permute-start | bytes 196616 | tf_op jit(solution)/shard_map/ppermute | solution.py:327
  10.7 10.0 %collective-permute-start.1 = (bf16[128,256]{1,0:T(8,128)(2,1)S(1)}, bf16[128,256]{1,0:T(8,128)(2,1)S(1)}, u32[]{:S(2)}, u32[]{:S(2)}) collective-permute-start(bf16[128,256]{1,0:T(8,128)(2,1)S(1)} %get-tuple-element.45), channel_id=1, source_target_pairs={{0,8},{1,9},{2,10},{3,11},{4,12},{5,13},{6,14},{7,15},{8,0},{9,1},... | collective-permute-start | bytes 196616 | tf_op jit(solution)/shard_map/ppermute | solution.py:327
  13.4 7.3 %collective-permute-start.2 = (bf16[128,256]{1,0:T(8,128)(2,1)S(1)}, bf16[128,256]{1,0:T(8,128)(2,1)S(1)}, u32[]{:S(2)}, u32[]{:S(2)}) collective-permute-start(bf16[128,256]{1,0:T(8,128)(2,1)S(1)} %get-tuple-element.45), channel_id=1, source_target_pairs={{0,12},{1,13},{2,14},{3,15},{4,0},{5,1},{6,2},{7,3},{8,4},{9,5},{1... | collective-permute-start | bytes 196616 | tf_op jit(solution)/shard_map/ppermute | solution.py:327
  14.8 6.1 %collective-permute-start.3 = (bf16[128,256]{1,0:T(8,128)(2,1)S(1)}, bf16[128,256]{1,0:T(8,128)(2,1)S(1)}, u32[]{:S(2)}, u32[]{:S(2)}) collective-permute-start(bf16[128,256]{1,0:T(8,128)(2,1)S(1)} %get-tuple-element.49), channel_id=1, source_target_pairs={{0,1},{1,2},{2,3},{3,0},{4,5},{5,6},{6,7},{7,4},{8,9},{9,10},{10,1... | collective-permute-start | bytes 196616 | tf_op jit(solution)/shard_map/ppermute | solution.py:327
  16.4 5.8 %collective-permute-start.4 = (bf16[128,256]{1,0:T(8,128)(2,1)S(1)}, bf16[128,256]{1,0:T(8,128)(2,1)S(1)}, u32[]{:S(2)}, u32[]{:S(2)}) collective-permute-start(bf16[128,256]{1,0:T(8,128)(2,1)S(1)} %get-tuple-element.49), channel_id=1, source_target_pairs={{0,2},{1,3},{2,0},{3,1},{4,6},{5,7},{6,4},{7,5},{8,10},{9,11},{10,... | collective-permute-start | bytes 196616 | tf_op jit(solution)/shard_map/ppermute | solution.py:327
  19.3 4.3 %collective-permute-start.5 = (bf16[128,256]{1,0:T(8,128)(2,1)S(1)}, bf16[128,256]{1,0:T(8,128)(2,1)S(1)}, u32[]{:S(2)}, u32[]{:S(2)}) collective-permute-start(bf16[128,256]{1,0:T(8,128)(2,1)S(1)} %get-tuple-element.49), channel_id=1, source_target_pairs={{0,3},{1,0},{2,1},{3,2},{4,7},{5,4},{6,5},{7,6},{8,11},{9,8},{10,9... | collective-permute-start | bytes 196616 | tf_op jit(solution)/shard_map/ppermute | solution.py:327
  23.6 9.4 %collective-permute-start.10 = (bf16[512,256]{1,0:T(8,128)(2,1)S(1)}, bf16[512,256]{1,0:T(8,128)(2,1)S(1)}, u32[]{:S(2)}, u32[]{:S(2)}) collective-permute-start(bf16[512,256]{1,0:T(8,128)(2,1)S(1)} %get-tuple-element.59.refs_4_), channel_id=1, source_target_pairs={{0,8},{1,9},{2,10},{3,11},{4,12},{5,13},{6,14},{7,15},{8,0},{9,1},... | collective-permute-start | bytes 786440 | tf_op jit(solution)/shard_map/ppermute | solution.py:327
  24.2 25.4 %collective-permute-start.11 = (bf16[512,256]{1,0:T(8,128)(2,1)S(1)}, bf16[512,256]{1,0:T(8,128)(2,1)S(1)}, u32[]{:S(2)}, u32[]{:S(2)}) collective-permute-start(bf16[512,256]{1,0:T(8,128)(2,1)S(1)} %get-tuple-element.59.refs_4_), channel_id=1, source_target_pairs={{0,12},{1,13},{2,14},{3,15},{4,0},{5,1},{6,2},{7,3},{8,4},{9,5},{1... | collective-permute-start | bytes 786440 | tf_op jit(solution)/shard_map/ppermute | solution.py:327
  27.0 22.6 %collective-permute-start.6 = (bf16[512,256]{1,0:T(8,128)(2,1)S(1)}, bf16[512,256]{1,0:T(8,128)(2,1)S(1)}, u32[]{:S(2)}, u32[]{:S(2)}) collective-permute-start(bf16[512,256]{1,0:T(8,128)(2,1)S(1)} %get-tuple-element.55.refs_0_), channel_id=1, source_target_pairs={{0,1},{1,2},{2,3},{3,0},{4,5},{5,6},{6,7},{7,4},{8,9},{9,10},{10,1... | collective-permute-start | bytes 786440 | tf_op jit(solution)/shard_map/ppermute | solution.py:327
  27.3 22.3 %collective-permute-start.7 = (bf16[512,256]{1,0:T(8,128)(2,1)S(1)}, bf16[512,256]{1,0:T(8,128)(2,1)S(1)}, u32[]{:S(2)}, u32[]{:S(2)}) collective-permute-start(bf16[512,256]{1,0:T(8,128)(2,1)S(1)} %get-tuple-element.55.refs_0_), channel_id=1, source_target_pairs={{0,2},{1,3},{2,0},{3,1},{4,6},{5,7},{6,4},{7,5},{8,10},{9,11},{10,... | collective-permute-start | bytes 786440 | tf_op jit(solution)/shard_map/ppermute | solution.py:327
  31.0 18.6 %collective-permute-start.8 = (bf16[512,256]{1,0:T(8,128)(2,1)S(1)}, bf16[512,256]{1,0:T(8,128)(2,1)S(1)}, u32[]{:S(2)}, u32[]{:S(2)}) collective-permute-start(bf16[512,256]{1,0:T(8,128)(2,1)S(1)} %get-tuple-element.55.refs_0_), channel_id=1, source_target_pairs={{0,3},{1,0},{2,1},{3,2},{4,7},{5,4},{6,5},{7,6},{8,11},{9,8},{10,9... | collective-permute-start | bytes 786440 | tf_op jit(solution)/shard_map/ppermute | solution.py:327
  33.0 16.6 %collective-permute-start.9 = (bf16[512,256]{1,0:T(8,128)(2,1)S(1)}, bf16[512,256]{1,0:T(8,128)(2,1)S(1)}, u32[]{:S(2)}, u32[]{:S(2)}) collective-permute-start(bf16[512,256]{1,0:T(8,128)(2,1)S(1)} %get-tuple-element.59.refs_4_), channel_id=1, source_target_pairs={{0,4},{1,5},{2,6},{3,7},{4,8},{5,9},{6,10},{7,11},{8,12},{9,13},{1... | collective-permute-start | bytes 786440 | tf_op jit(solution)/shard_map/ppermute | solution.py:327
  63.5 33.1 %all-to-all-start.1 = ((bf16[16,528,128]{2,1,0:T(8,128)(2,1)}), bf16[16,528,128]{2,1,0:T(8,128)(2,1)S(1)}, u32[]{:S(2)}, u32[]{:S(2)}) async-start(bf16[16,528,128]{2,1,0:T(8,128)(2,1)} %attend.3), calls=%async_computation.1 | async-start | bytes 4325376 | tf_op jit(solution)/shard_map/all_to_all | solution.py:306
  97.9 32.6 %all-to-all-start = ((bf16[16,528,128]{2,1,0:T(8,128)(2,1)}), bf16[16,528,128]{2,1,0:T(8,128)(2,1)S(1)}, u32[]{:S(2)}, u32[]{:S(2)}) async-start(bf16[16,528,128]{2,1,0:T(8,128)(2,1)} %attend.2), calls=%async_computation | async-start | bytes 4325376 | tf_op jit(solution)/shard_map/all_to_all | solution.py:306
  102.0 1.6 %copy-start.1 = (bf16[16,528,128]{2,1,0:T(8,128)(2,1)S(1)}, bf16[16,528,128]{2,1,0:T(8,128)(2,1)}, u32[]{:S(2)}) copy-start(bf16[16,528,128]{2,1,0:T(8,128)(2,1)} %copy-done) | copy-start | bytes 6488068
  108.6 2.1 %collective-permute-start.12 = (bf16[4,128,512]{2,1,0:T(8,128)(2,1)}, bf16[4,128,512]{2,1,0:T(8,128)(2,1)S(1)}, u32[]{:S(2)}, u32[]{:S(2)}) collective-permute-start(bf16[4,128,512]{2,1,0:T(8,128)(2,1)} %get-tuple-element.64), channel_id=1, source_target_pairs={{0,16},{16,0},{32,48},{48,32},{64,80},{80,64},{96,112},{112,96},{1... | collective-permute-start | bytes 1572872 | tf_op jit(solution)/shard_map/ppermute | solution.py:311
  110.8 8.7 %collective-permute-start.13 = (bf16[128,512]{1,0:T(8,128)(2,1)S(1)}, bf16[128,512]{1,0:T(8,128)(2,1)S(1)}, u32[]{:S(2)}, u32[]{:S(2)}) collective-permute-start(bf16[128,512]{1,0:T(8,128)(2,1)S(1)} %get-tuple-element.66), channel_id=1, source_target_pairs={{0,32},{16,48},{32,64},{48,80},{64,96},{80,112},{96,0},{112,16},{1... | collective-permute-start | bytes 393224 | tf_op jit(solution)/shard_map/ppermute | solution.py:315
  112.8 9.0 %collective-permute-start.14 = (bf16[128,512]{1,0:T(8,128)(2,1)S(1)}, bf16[128,512]{1,0:T(8,128)(2,1)S(1)}, u32[]{:S(2)}, u32[]{:S(2)}) collective-permute-start(bf16[128,512]{1,0:T(8,128)(2,1)S(1)} %get-tuple-element.67), channel_id=1, source_target_pairs={{0,96},{16,112},{32,0},{48,16},{64,32},{80,48},{96,64},{112,80},{1... | collective-permute-start | bytes 393224 | tf_op jit(solution)/shard_map/ppermute | solution.py:315
  114.1 10.0 %collective-permute-start.15 = (bf16[128,512]{1,0:T(8,128)(2,1)S(1)}, bf16[128,512]{1,0:T(8,128)(2,1)S(1)}, u32[]{:S(2)}, u32[]{:S(2)}) collective-permute-start(bf16[128,512]{1,0:T(8,128)(2,1)S(1)} %get-tuple-element.68), channel_id=1, source_target_pairs={{0,64},{16,80},{32,96},{48,112},{64,0},{80,16},{96,32},{112,48},{1... | collective-permute-start | bytes 393224 | tf_op jit(solution)/shard_map/ppermute | solution.py:315
  134.6 2.0 %collective-permute-start.16 = (bf16[4,128,512]{2,1,0:T(8,128)(2,1)S(1)}, bf16[4,128,512]{2,1,0:T(8,128)(2,1)S(1)}, u32[]{:S(2)}, u32[]{:S(2)}) collective-permute-start(bf16[4,128,512]{2,1,0:T(8,128)(2,1)S(1)} %get-tuple-element.72), channel_id=1, source_target_pairs={{0,16},{16,0},{32,48},{48,32},{64,80},{80,64},{96,112},{112,96},{1... | collective-permute-start | bytes 1572872 | tf_op jit(solution)/shard_map/ppermute | solution.py:311
  136.7 8.5 %collective-permute-start.17 = (bf16[128,512]{1,0:T(8,128)(2,1)S(1)}, bf16[128,512]{1,0:T(8,128)(2,1)S(1)}, u32[]{:S(2)}, u32[]{:S(2)}) collective-permute-start(bf16[128,512]{1,0:T(8,128)(2,1)S(1)} %get-tuple-element.74), channel_id=1, source_target_pairs={{0,32},{16,48},{32,64},{48,80},{64,96},{80,112},{96,0},{112,16},{1... | collective-permute-start | bytes 393224 | tf_op jit(solution)/shard_map/ppermute | solution.py:315
  136.8 10.7 %collective-permute-start.18 = (bf16[128,512]{1,0:T(8,128)(2,1)S(1)}, bf16[128,512]{1,0:T(8,128)(2,1)S(1)}, u32[]{:S(2)}, u32[]{:S(2)}) collective-permute-start(bf16[128,512]{1,0:T(8,128)(2,1)S(1)} %get-tuple-element.75), channel_id=1, source_target_pairs={{0,96},{16,112},{32,0},{48,16},{64,32},{80,48},{96,64},{112,80},{1... | collective-permute-start | bytes 393224 | tf_op jit(solution)/shard_map/ppermute | solution.py:315
  140.1 9.8 %collective-permute-start.19 = (bf16[128,512]{1,0:T(8,128)(2,1)S(1)}, bf16[128,512]{1,0:T(8,128)(2,1)S(1)}, u32[]{:S(2)}, u32[]{:S(2)}) collective-permute-start(bf16[128,512]{1,0:T(8,128)(2,1)S(1)} %get-tuple-element.76), channel_id=1, source_target_pairs={{0,64},{16,80},{32,96},{48,112},{64,0},{80,16},{96,32},{112,48},{1... | collective-permute-start | bytes 393224 | tf_op jit(solution)/shard_map/ppermute | solution.py:315
  (2 other events, 2.0 us)
Sparse Core Ops, SparseCore 0:
  9.5 50.9 all-gather.1

commit v2 on v1

--- a/solution.py
+++ b/solution.py
@@ -10,6 +10,8 @@
 
 BLOCK = 128
 UNROLL = 16
+PLAN_UNROLL = 8
+CHUNK_BIT = 28
 STAT_ROWS = 16
 ABSENT = -3.0e38
 Z_STEPS = (1, 3, 2)
@@ -24,60 +26,65 @@
     return high, middle, rest - middle
 
 
-def plan_kernel(tiles, owned, side, me, ids, counts, entries, starts):
-    heads = ids.shape[0]
-    my_x = lax.div(me[0], jnp.int32(side))
-    my_y = lax.rem(me[0], jnp.int32(side))
-    zero = jnp.int32(0)
+def plan_kernel(owned, codes, counts, entries, starts):
+    heads = codes.shape[0]
 
     def over_head(h, at):
         for c in range(owned):
             starts[c, h] = at[c]
-
-        def one(j, at):
-            block = ids[h, j]
-            query = lax.div(block, jnp.int32(tiles))
-            tile = lax.rem(block, jnp.int32(tiles))
-            chunk = lax.rem(query, jnp.int32(owned))
-            owner = lax.div(query, jnp.int32(owned))
-            dx = lax.rem(my_x - lax.div(owner, jnp.int32(side)) + side, jnp.int32(side))
-            dy = lax.rem(my_y - lax.rem(owner, jnp.int32(side)) + side, jnp.int32(side))
-            near = jnp.where(h < heads // 2, dy * side + dx, dx * side + dy)
-            position = jnp.where(chunk == 0, near, owner)
-            place = at[0]
-            for c in range(1, owned):
-                place = jnp.where(chunk == c, at[c], place)
-            entries[chunk, place] = ((h * 256 + owner) * 256 + position) * 256 + tile
-            return tuple(a + jnp.where(chunk == c, 1, 0) for c, a in enumerate(at))
-
-        return lax.fori_loop(0, counts[h, 0], one, at)
-
-    at = lax.fori_loop(0, heads, over_head, (zero,) * owned)
+        count = counts[h, 0]
+
+        def some(step, at):
+            for u in range(PLAN_UNROLL):
+                j = step * PLAN_UNROLL + u
+                code = codes[h, j]
+                chunk = lax.shift_right_logical(code, CHUNK_BIT)
+                place = at[0]
+                for c in range(1, owned):
+                    place = jnp.where(chunk == c, at[c], place)
+                entries[chunk, place] = code
+                live = j < count
+                at = tuple(
+                    a + jnp.where(live & (chunk == c), 1, 0) for c, a in enumerate(at)
+                )
+            return at
+
+        return lax.fori_loop(0, lax.div(count + PLAN_UNROLL - 1, PLAN_UNROLL), some, at)
+
+    at = lax.fori_loop(0, heads, over_head, (jnp.int32(0),) * owned)
     for c in range(owned):
         starts[c, heads] = at[c]
 
 
 def plan(me, ids, counts, tiles, owned, side):
     heads, slots = ids.shape
+    query, tile = ids // tiles, ids % tiles
+    owner, chunk = query // owned, query % owned
+    dx = (me // side - owner // side) % side
+    dy = (me % side - owner % side) % side
+    head = jnp.arange(heads, dtype=jnp.int32)[:, None]
+    near = jnp.where(head < heads // 2, dy * side + dx, dx * side + dy)
+    position = jnp.where(chunk == 0, near, owner)
+    codes = (((chunk * 16 + head) * 256 + owner) * 256 + position) * 256 + tile
     smem = pl.BlockSpec(memory_space=pltpu.SMEM)
     return pl.pallas_call(
-        functools.partial(plan_kernel, tiles, owned, side),
+        functools.partial(plan_kernel, owned),
         out_shape=(
-            jax.ShapeDtypeStruct((owned, heads * slots), jnp.int32),
+            jax.ShapeDtypeStruct((owned, heads * slots + PLAN_UNROLL), jnp.int32),
             jax.ShapeDtypeStruct((owned, heads + 1), jnp.int32),
         ),
-        in_specs=[smem, smem, smem],
+        in_specs=[smem, smem],
         out_specs=(smem, smem),
         compiler_params=pltpu.CompilerParams(vmem_limit_bytes=1024 * 1024),
         name="plan",
-    )(me, ids, counts)
+    )(codes, counts)
 
 
 def attend_kernel(chunk, sources, entries, starts, *refs):
     blocks = 1 + max(i for pieces in sources for i, _ in pieces)
     q_hbm = refs[:blocks]
     k_hbm, v_hbm, out_ref, qs, ks, vs, acc, top, den, stats, sems = refs[blocks:]
-    heads, _, width = ks.shape
+    heads, _, width = qs.shape
     owners = qs.shape[1] // BLOCK
     scale = width**-0.5 * math.log2(math.e)
 
@@ -115,7 +122,7 @@
             j = step * UNROLL + u
             live = j < count
             entry = jnp.where(live, entries[chunk, j], 0)
-            head = lax.shift_right_logical(entry, 24)
+            head = lax.bitwise_and(lax.shift_right_logical(entry, 24), 15)
             owner = lax.bitwise_and(lax.shift_right_logical(entry, 16), 255)
             position = lax.bitwise_and(lax.shift_right_logical(entry, 8), 255)
             tile = lax.bitwise_and(entry, 255)
@@ -134,11 +141,18 @@
             )
             for _, head, position, tile in slots
         ]
+        scores = [s * scale for s in scores]
+        tops = [jnp.max(s, axis=0, keepdims=True) for s in scores]
+        steps = []
+        for (slot, _, _, _), m in zip(slots, tops):
+            row = pl.ds(slot, 1)
+            old = top[row, :]
+            new = jnp.maximum(old, m)
+            top[row, :] = new
+            steps.append((new, jnp.exp2(old - new)))
         parts = []
-        for (slot, head, _, tile), s in zip(slots, scores):
-            s = s * scale
-            m = jnp.max(s, axis=0, keepdims=True)
-            p = jnp.exp2(s - m)
+        for (slot, head, _, tile), s, (new, _) in zip(slots, scores, steps):
+            p = jnp.exp2(s - new)
             d = jnp.sum(p, axis=0, keepdims=True)
             o = lax.dot_general(
                 vs[head, rows(tile), :],
@@ -146,16 +160,11 @@
                 (((0,), (0,)), ((), ())),
                 preferred_element_type=F32,
             )
-            parts.append((slot, m, d, o))
-        for slot, m, d, o in parts:
+            parts.append((d, o))
+        for (slot, _, _, _), (_, keep), (d, o) in zip(slots, steps, parts):
             row = pl.ds(slot, 1)
-            old = top[row, :]
-            new = jnp.maximum(old, m)
-            keep = jnp.exp2(old - new)
-            take = jnp.exp2(m - new)
-            top[row, :] = new
-            den[row, :] = den[row, :] * keep + d * take
-            acc[slot] = acc[slot] * keep + o * take
+            den[row, :] = den[row, :] * keep + d
+            acc[slot] = acc[slot] * keep + o
         return carry
 
     lax.fori_loop(0, groups, group, 0)
@@ -211,31 +220,39 @@
             pltpu.VMEM((3 * heads, owners, BLOCK), F32),
             pltpu.SemaphoreType.DMA((heads, 2 + max(len(p) for p in sources))),
         ],
-        compiler_params=pltpu.CompilerParams(vmem_limit_bytes=48 * 1024 * 1024),
+        compiler_params=pltpu.CompilerParams(vmem_limit_bytes=40 * 1024 * 1024),
         name="attend",
     )(entries, starts, *queries, in_hbm(keys), in_hbm(values))
 
 
-def project_kernel(heads, core, in_ref, own_weight, other_weight, own_ref, other_ref, mixed):
+def project_kernel(heads, core, in_ref, weight, own_ref, other_ref, mixed, held, sems):
     ranges, total, rows = in_ref.shape
     width = (total - STAT_ROWS) // heads
     first = total - STAT_ROWS
-
-    @pl.when(pl.program_id(0) == 0)
-    def _():
-        stats = in_ref[:, first:, :].astype(F32)
-        for h in range(heads):
-            level = stats[:, 3 * h, :] + stats[:, 3 * h + 1, :] + stats[:, 3 * h + 2, :]
-            share = jnp.exp2(level - jnp.max(level, axis=0, keepdims=True))
-            share = share / jnp.sum(share, axis=0, keepdims=True)
-            acc = jnp.zeros((width, rows), F32)
-            for r in range(ranges):
-                acc += in_ref[r, h * width : (h + 1) * width, :].astype(F32) * share[r : r + 1, :]
-            mixed[h * width : (h + 1) * width, :] = acc.astype(BF16)
-
-    for weight, out_ref in ((own_weight, own_ref), (other_weight, other_ref)):
-        out_ref[0] = lax.dot_general(
-            mixed[...], weight[...], (((0,), (0,)), ((), ())), preferred_element_type=F32
+    zs, _, span = own_ref.shape
+
+    def copy(z, s):
+        column = pl.multiple_of((2 * z + jnp.bitwise_xor(core[0], s)) * span, span)
+        return pltpu.make_async_copy(
+            weight.at[:, pl.ds(column, span)], held.at[z, s], sems.at[z, s]
+        )
+
+    turns = [(z, s) for z in range(zs) for s in range(2)]
+    for z, s in turns:
+        copy(z, s).start()
+    stats = in_ref[:, first:, :].astype(F32)
+    for h in range(heads):
+        level = stats[:, 3 * h, :] + stats[:, 3 * h + 1, :] + stats[:, 3 * h + 2, :]
+        share = jnp.exp2(level - jnp.max(level, axis=0, keepdims=True))
+        share = share / jnp.sum(share, axis=0, keepdims=True)
+        acc = jnp.zeros((width, rows), F32)
+        for r in range(ranges):
+            acc += in_ref[r, h * width : (h + 1) * width, :].astype(F32) * share[r : r + 1, :]
+        mixed[h * width : (h + 1) * width, :] = acc.astype(BF16)
+    for z, s in turns:
+        copy(z, s).wait()
+        (own_ref, other_ref)[s][z] = lax.dot_general(
+            mixed[...], held[z, s], (((0,), (0,)), ((), ())), preferred_element_type=F32
         ).astype(BF16)
 
 
@@ -243,26 +260,27 @@
     depth = weight.shape[0]
     zs = weight.shape[1] // span // 2
     rows = parts.shape[2]
-    result = pl.BlockSpec((1, rows, span), lambda z, core: (z, 0, 0))
+    result = pl.BlockSpec((zs, rows, span), lambda i, core: (0, 0, 0))
     return pl.pallas_call(
         functools.partial(project_kernel, heads),
         out_shape=[jax.ShapeDtypeStruct((zs, rows, span), BF16)] * 2,
         grid_spec=pltpu.PrefetchScalarGridSpec(
             num_scalar_prefetch=1,
-            grid=(zs,),
+            grid=(1,),
             in_specs=[
-                pl.BlockSpec(parts.shape, lambda z, core: (0, 0, 0)),
-                pl.BlockSpec((depth, span), lambda z, core: (0, 2 * z + core[0])),
-                pl.BlockSpec((depth, span), lambda z, core: (0, 2 * z + 1 - core[0])),
+                pl.BlockSpec(parts.shape, lambda i, core: (0, 0, 0)),
+                pl.BlockSpec(memory_space=pl.ANY),
             ],
             out_specs=[result, result],
-            scratch_shapes=[pltpu.VMEM((depth, rows), BF16)],
+            scratch_shapes=[
+                pltpu.VMEM((depth, rows), BF16),
+                pltpu.VMEM((zs, 2, depth, span), BF16),
+                pltpu.SemaphoreType.DMA((zs, 2)),
+            ],
         ),
-        compiler_params=pltpu.CompilerParams(
-            dimension_semantics=("arbitrary",), vmem_limit_bytes=32 * 1024 * 1024
-        ),
+        compiler_params=pltpu.CompilerParams(vmem_limit_bytes=24 * 1024 * 1024),
         name="project",
-    )(core, parts, in_hbm(weight), in_hbm(weight))
+    )(core, parts, in_hbm(weight))
 
 
 def pair_kernel(z, mine, theirs, own, *others):

time: 157 us -> 150 us (0.955); the launches traced: 157 us -> 148 us
  Pallas kernels: 48 us -> 37.7 us
  waiting for transfers between devices: 40.1 us -> 48.8 us
  starting transfers between devices: 48.1 us -> 40.4 us
    pallas_call x1, Pallas kernels: 11.8 us -> 4.59 us  [plan(): pl.pallas_call(functools.partial(plan_kernel, owned), out_shape=(jax.Shap...]
    ppermute x6, starting transfers between devices: 17.2 us -> 10.1 us  [finish(): total = total + lax.ppermute(piece, 'heads', pairs).astype(F32)]
    all_to_all x2, waiting for transfers between devices: 22.1 us -> 28.8 us  [exchange(): lax.all_to_all(parts, 'keys', split_axis=0, concat_axis=0, tiled=True)]
    pallas_call x2, Pallas kernels: 9.09 us -> 7.14 us  [project(): pl.pallas_call(functools.partial(project_kernel, heads), out_shape=[jax.S...]
    unnamed x7 -> x5, local copies, waits for them, and re-layouts: 4.37 us -> 3.69 us
  transfers between devices with their start and end apart: 23 -> 23, of which waited for: 12 -> 15; matrix products, arithmetic and copies ran while one was open for 1% -> 2% of each run, Pallas kernels for 28% -> 23%
where the time goes in v2:
time: 150 us; the launch traced here: 148 us
  waiting for transfers between devices  48.8 us (33%)
  starting transfers between devices  40.4 us (27%)
  Pallas kernels  37.7 us (25%)
  between operations  13.6 us (9%)
  local copies, waits for them, and re-layouts  6.14 us (4%)
  other arithmetic  1.65 us (1%)
    all_to_all x2, waiting for transfers between devices, exchange(): lax.all_to_all(parts, 'keys', split_axis=0, concat_axis=0, tiled=True)  28.8 us
    pallas_call x2, Pallas kernels, attend(): pl.pallas_call(functools.partial(attend_kernel, chunk, sources), out_shap...  25.8 us
    ppermute x12, starting transfers between devices, along(): got = {d: lax.ppermute(x, 'keys', pairs(d)) for d in Z_STEPS}  22.4 us
    ppermute x6, waiting for transfers between devices, finish(): total = total + lax.ppermute(piece, 'heads', pairs).astype(F32)  10.2 us
    ppermute x6, starting transfers between devices, finish(): total = total + lax.ppermute(piece, 'heads', pairs).astype(F32)  10.1 us
    all_to_all x2, starting transfers between devices, exchange(): lax.all_to_all(parts, 'keys', split_axis=0, concat_axis=0, tiled=True)  7.72 us
    pallas_call x2, Pallas kernels, project(): pl.pallas_call(functools.partial(project_kernel, heads), out_shape=[jax.S...  7.14 us
    ppermute x12, waiting for transfers between devices, along(): got = {d: lax.ppermute(x, 'keys', pairs(d)) for d in Z_STEPS}  4.82 us
  transfers between devices with their start and end apart: 23, of which 15 were waited for; matrix products, arithmetic and copies ran while one was open for 2% of the time, Pallas kernels for 23%

profile of v2, /device:TPU:0, one launch (start us, length us, event | category | flops | bytes accessed | tf_op | source)
XLA Modules:
  0.0 148.4 jit_solution(16443857248841086929)
XLA Ops:
  9.0 1.6 %collective-permute-start = (bf16[128,256]{1,0:T(8,128)(2,1)S(1)}, bf16[128,256]{1,0:T(8,128)(2,1)S(1)}, u32[]{:S(2)}, u32[]{:S(2)}) collective-permute-start(bf16[128,256]{1,0:T(8,128)(2,1)S(1)} %get-tuple-element.45), channel_id=1, source_target_pairs={{0,4},{1,5},{2,6},{3,7},{4,8},{5,9},{6,10},{7,11},{8,12},{9,13},{1... | collective-permute-start | bytes 196616 | tf_op jit(solution)/shard_map/ppermute | solution.py:345
  10.7 2.7 %collective-permute-start.1 = (bf16[128,256]{1,0:T(8,128)(2,1)S(1)}, bf16[128,256]{1,0:T(8,128)(2,1)S(1)}, u32[]{:S(2)}, u32[]{:S(2)}) collective-permute-start(bf16[128,256]{1,0:T(8,128)(2,1)S(1)} %get-tuple-element.45), channel_id=1, source_target_pairs={{0,8},{1,9},{2,10},{3,11},{4,12},{5,13},{6,14},{7,15},{8,0},{9,1},... | collective-permute-start | bytes 196616 | tf_op jit(solution)/shard_map/ppermute | solution.py:345
  16.4 2.9 %collective-permute-start.4 = (bf16[128,256]{1,0:T(8,128)(2,1)S(1)}, bf16[128,256]{1,0:T(8,128)(2,1)S(1)}, u32[]{:S(2)}, u32[]{:S(2)}) collective-permute-start(bf16[128,256]{1,0:T(8,128)(2,1)S(1)} %get-tuple-element.49), channel_id=1, source_target_pairs={{0,2},{1,3},{2,0},{3,1},{4,6},{5,7},{6,4},{7,5},{8,10},{9,11},{10,... | collective-permute-start | bytes 196616 | tf_op jit(solution)/shard_map/ppermute | solution.py:345
  24.2 2.8 %collective-permute-start.11 = (bf16[512,256]{1,0:T(8,128)(2,1)S(1)}, bf16[512,256]{1,0:T(8,128)(2,1)S(1)}, u32[]{:S(2)}, u32[]{:S(2)}) collective-permute-start(bf16[512,256]{1,0:T(8,128)(2,1)S(1)} %get-tuple-element.59.refs_4_), channel_id=1, source_target_pairs={{0,12},{1,13},{2,14},{3,15},{4,0},{5,1},{6,2},{7,3},{8,4},{9,5},{1... | collective-permute-start | bytes 786440 | tf_op jit(solution)/shard_map/ppermute | solution.py:345
  27.3 3.7 %collective-permute-start.7 = (bf16[512,256]{1,0:T(8,128)(2,1)S(1)}, bf16[512,256]{1,0:T(8,128)(2,1)S(1)}, u32[]{:S(2)}, u32[]{:S(2)}) collective-permute-start(bf16[512,256]{1,0:T(8,128)(2,1)S(1)} %get-tuple-element.55.refs_0_), channel_id=1, source_target_pairs={{0,2},{1,3},{2,0},{3,1},{4,6},{5,7},{6,4},{7,5},{8,10},{9,11},{10,... | collective-permute-start | bytes 786440 | tf_op jit(solution)/shard_map/ppermute | solution.py:345
  31.1 1.9 %collective-permute-done.10.refs_6_ = bf16[512,256]{1,0:T(8,128)(2,1)S(1)} collective-permute-done((bf16[512,256]{1,0:T(8,128)(2,1)S(1)}, bf16[512,256]{1,0:T(8,128)(2,1)S(1)}, u32[]{:S(2)}, u32[]{:S(2)}) %collective-permute-start.10) | collective-permute-done | bytes 262176 | tf_op jit(solution)/shard_map/ppermute | solution.py:345
  33.0 3.3 %collective-permute-start.9 = (bf16[512,256]{1,0:T(8,128)(2,1)S(1)}, bf16[512,256]{1,0:T(8,128)(2,1)S(1)}, u32[]{:S(2)}, u32[]{:S(2)}) collective-permute-start(bf16[512,256]{1,0:T(8,128)(2,1)S(1)} %get-tuple-element.59.refs_4_), channel_id=1, source_target_pairs={{0,4},{1,5},{2,6},{3,7},{4,8},{5,9},{6,10},{7,11},{8,12},{9,13},{1... | collective-permute-start | bytes 786440 | tf_op jit(solution)/shard_map/ppermute | solution.py:345
  37.8 4.6 %plan.1 = (s32[2,776]{1,0:T(2,128)S(1)}, s32[2,5]{1,0:T(2,128)S(1)}) custom-call(s32[4,192]{1,0:T(4,128)S(1)} %fusion.4.codes, s32[4,1]{1,0:T(4,128)S(1)} %copy.7.counts), custom_call_target="tpu_custom_call" | custom-call | tf_op jit(solution)/shard_map/plan/pallas_call | solution.py:70
  42.4 13.1 %attend.3 = bf16[16,528,128]{2,1,0:T(8,128)(2,1)} custom-call(s32[2,776]{1,0:T(2,128)S(1)} %get-tuple-element.41.entries, s32[2,5]{1,0:T(2,128)S(1)} %get-tuple-element.42.starts, bf16[512,256]{1,0:T(8,128)(2,1)S(1)} %get-tuple-element.55.refs_0_, bf16[512,256]{1,0:T(8,128)(2,1)S(1)} %collective-permute-done.6.refs_1_, ...), custom_call_target="tpu_custom_call" | custom-call | tf_op jit(solution)/shard_map/attend/pallas_call | solution.py:209
  55.5 4.0 %all-to-all-start.1 = ((bf16[16,528,128]{2,1,0:T(8,128)(2,1)}), bf16[16,528,128]{2,1,0:T(8,128)(2,1)S(1)}, u32[]{:S(2)}, u32[]{:S(2)}) async-start(bf16[16,528,128]{2,1,0:T(8,128)(2,1)} %attend.3), calls=%async_computation.1 | async-start | bytes 4325376 | tf_op jit(solution)/shard_map/all_to_all | solution.py:324
  60.5 12.7 %attend.2 = bf16[16,528,128]{2,1,0:T(8,128)(2,1)} custom-call(s32[2,776]{1,0:T(2,128)S(1)} %get-tuple-element.41.entries, s32[2,5]{1,0:T(2,128)S(1)} %get-tuple-element.42.starts, bf16[2048,512]{1,0:T(8,128)(2,1)} %all-gather.2.cloned.1.call-done.refs_0_, bf16[8192,512]{1,0:T(8,128)(2,1)} %refs_8_.1, bf16[8192,512]{1,0:T(8,128)(2,1)} %refs_9_.1), custom_call_target="tpu_custom_call" | custom-call | tf_op jit(solution)/shard_map/attend/pallas_call | solution.py:209
  73.2 17.8 %all-to-all-done.1.in_ref = bf16[16,528,128]{2,1,0:T(8,128)(2,1)S(1)} async-done(((bf16[16,528,128]{2,1,0:T(8,128)(2,1)}), bf16[16,528,128]{2,1,0:T(8,128)(2,1)S(1)}, u32[]{:S(2)}, u32[]{:S(2)}) %all-to-all-start.1) | async-done | bytes 2162720 | tf_op jit(solution)/shard_map/all_to_all | solution.py:324
  92.3 3.7 %all-to-all-start = ((bf16[16,528,128]{2,1,0:T(8,128)(2,1)}), bf16[16,528,128]{2,1,0:T(8,128)(2,1)S(1)}, u32[]{:S(2)}, u32[]{:S(2)}) async-start(bf16[16,528,128]{2,1,0:T(8,128)(2,1)} %attend.2), calls=%async_computation | async-start | bytes 4325376 | tf_op jit(solution)/shard_map/all_to_all | solution.py:324
  97.7 4.0 %project.2 = (bf16[4,128,512]{2,1,0:T(8,128)(2,1)S(1)}, bf16[4,128,512]{2,1,0:T(8,128)(2,1)}) custom-call(s32[1]{0:T(128)} %bitcast.4.core, bf16[16,528,128]{2,1,0:T(8,128)(2,1)S(1)} %copy-done.1, bf16[512,4096]{1,0:T(8,128)(2,1)} %weight.3), custom_call_target="tpu_custom_call" | custom-call | tf_op jit(solution)/shard_map/project/pallas_call | solution.py:264
  101.8 2.1 %collective-permute-done.12.theirs = bf16[4,128,512]{2,1,0:T(8,128)(2,1)S(1)} collective-permute-done((bf16[4,128,512]{2,1,0:T(8,128)(2,1)}, bf16[4,128,512]{2,1,0:T(8,128)(2,1)S(1)}, u32[]{:S(2)}, u32[]{:S(2)}) %collective-permute-start.12) | collective-permute-done | bytes 524320 | tf_op jit(solution)/shard_map/ppermute | solution.py:329
  104.1 3.2 %collective-permute-start.14 = (bf16[128,512]{1,0:T(8,128)(2,1)S(1)}, bf16[128,512]{1,0:T(8,128)(2,1)S(1)}, u32[]{:S(2)}, u32[]{:S(2)}) collective-permute-start(bf16[128,512]{1,0:T(8,128)(2,1)S(1)} %get-tuple-element.67), channel_id=1, source_target_pairs={{0,96},{16,112},{32,0},{48,16},{64,32},{80,48},{96,64},{112,80},{1... | collective-permute-start | bytes 393224 | tf_op jit(solution)/shard_map/ppermute | solution.py:333
  108.3 2.5 %collective-permute-done.13 = bf16[128,512]{1,0:T(8,128)(2,1)S(1)} collective-permute-done((bf16[128,512]{1,0:T(8,128)(2,1)S(1)}, bf16[128,512]{1,0:T(8,128)(2,1)S(1)}, u32[]{:S(2)}, u32[]{:S(2)}) %collective-permute-start.13) | collective-permute-done | bytes 131104 | tf_op jit(solution)/shard_map/ppermute | solution.py:333
  110.8 2.1 %collective-permute-done.14 = bf16[128,512]{1,0:T(8,128)(2,1)S(1)} collective-permute-done((bf16[128,512]{1,0:T(8,128)(2,1)S(1)}, bf16[128,512]{1,0:T(8,128)(2,1)S(1)}, u32[]{:S(2)}, u32[]{:S(2)}) %collective-permute-start.14) | collective-permute-done | bytes 131104 | tf_op jit(solution)/shard_map/ppermute | solution.py:333
  113.8 11.0 %all-to-all-done.in_ref = bf16[16,528,128]{2,1,0:T(8,128)(2,1)S(1)} async-done(((bf16[16,528,128]{2,1,0:T(8,128)(2,1)}), bf16[16,528,128]{2,1,0:T(8,128)(2,1)S(1)}, u32[]{:S(2)}, u32[]{:S(2)}) %all-to-all-start) | async-done | bytes 2162720 | tf_op jit(solution)/shard_map/all_to_all | solution.py:324
  124.8 3.2 %project.3 = (bf16[4,128,512]{2,1,0:T(8,128)(2,1)S(1)}, bf16[4,128,512]{2,1,0:T(8,128)(2,1)S(1)}) custom-call(s32[1]{0:T(128)} %bitcast.4.core, bf16[16,528,128]{2,1,0:T(8,128)(2,1)S(1)} %all-to-all-done.in_ref, bf16[512,4096]{1,0:T(8,128)(2,1)} %weight.3), custom_call_target="tpu_custom_call" | custom-call | tf_op jit(solution)/shard_map/project/pallas_call | solution.py:264
  128.1 1.9 %collective-permute-done.16.theirs = bf16[4,128,512]{2,1,0:T(8,128)(2,1)S(1)} collective-permute-done((bf16[4,128,512]{2,1,0:T(8,128)(2,1)S(1)}, bf16[4,128,512]{2,1,0:T(8,128)(2,1)S(1)}, u32[]{:S(2)}, u32[]{:S(2)}) %collective-permute-start.16) | collective-permute-done | bytes 524320 | tf_op jit(solution)/shard_map/ppermute | solution.py:329
  130.2 3.2 %collective-permute-start.18 = (bf16[128,512]{1,0:T(8,128)(2,1)S(1)}, bf16[128,512]{1,0:T(8,128)(2,1)S(1)}, u32[]{:S(2)}, u32[]{:S(2)}) collective-permute-start(bf16[128,512]{1,0:T(8,128)(2,1)S(1)} %get-tuple-element.75), channel_id=1, source_target_pairs={{0,96},{16,112},{32,0},{48,16},{64,32},{80,48},{96,64},{112,80},{1... | collective-permute-start | bytes 393224 | tf_op jit(solution)/shard_map/ppermute | solution.py:333
  133.4 2.5 %collective-permute-start.19 = (bf16[128,512]{1,0:T(8,128)(2,1)S(1)}, bf16[128,512]{1,0:T(8,128)(2,1)S(1)}, u32[]{:S(2)}, u32[]{:S(2)}) collective-permute-start(bf16[128,512]{1,0:T(8,128)(2,1)S(1)} %get-tuple-element.76), channel_id=1, source_target_pairs={{0,64},{16,80},{32,96},{48,112},{64,0},{80,16},{96,32},{112,48},{1... | collective-permute-start | bytes 393224 | tf_op jit(solution)/shard_map/ppermute | solution.py:333
  138.2 2.6 %collective-permute-done.19 = bf16[128,512]{1,0:T(8,128)(2,1)S(1)} collective-permute-done((bf16[128,512]{1,0:T(8,128)(2,1)S(1)}, bf16[128,512]{1,0:T(8,128)(2,1)S(1)}, u32[]{:S(2)}, u32[]{:S(2)}) %collective-permute-start.19) | collective-permute-done | bytes 131104 | tf_op jit(solution)/shard_map/ppermute | solution.py:333
  (43 shorter events, 21.8 us)
Async XLA Ops:
  6.5 54.0 %all-gather.2.cloned.1.call-start = ((), (), s32[]{:S(2)}) async-start(), calls=%async_computation.2 | async-start | bytes 2228224 | tf_op jit(solution)/shard_map/all_gather | solution.py:368
  9.0 10.3 %collective-permute-start = (bf16[128,256]{1,0:T(8,128)(2,1)S(1)}, bf16[128,256]{1,0:T(8,128)(2,1)S(1)}, u32[]{:S(2)}, u32[]{:S(2)}) collective-permute-start(bf16[128,256]{1,0:T(8,128)(2,1)S(1)} %get-tuple-element.45), channel_id=1, source_target_pairs={{0,4},{1,5},{2,6},{3,7},{4,8},{5,9},{6,10},{7,11},{8,12},{9,13},{1... | collective-permute-start | bytes 196616 | tf_op jit(solution)/shard_map/ppermute | solution.py:345
  10.7 10.0 %collective-permute-start.1 = (bf16[128,256]{1,0:T(8,128)(2,1)S(1)}, bf16[128,256]{1,0:T(8,128)(2,1)S(1)}, u32[]{:S(2)}, u32[]{:S(2)}) collective-permute-start(bf16[128,256]{1,0:T(8,128)(2,1)S(1)} %get-tuple-element.45), channel_id=1, source_target_pairs={{0,8},{1,9},{2,10},{3,11},{4,12},{5,13},{6,14},{7,15},{8,0},{9,1},... | collective-permute-start | bytes 196616 | tf_op jit(solution)/shard_map/ppermute | solution.py:345
  13.4 7.3 %collective-permute-start.2 = (bf16[128,256]{1,0:T(8,128)(2,1)S(1)}, bf16[128,256]{1,0:T(8,128)(2,1)S(1)}, u32[]{:S(2)}, u32[]{:S(2)}) collective-permute-start(bf16[128,256]{1,0:T(8,128)(2,1)S(1)} %get-tuple-element.45), channel_id=1, source_target_pairs={{0,12},{1,13},{2,14},{3,15},{4,0},{5,1},{6,2},{7,3},{8,4},{9,5},{1... | collective-permute-start | bytes 196616 | tf_op jit(solution)/shard_map/ppermute | solution.py:345
  14.8 6.1 %collective-permute-start.3 = (bf16[128,256]{1,0:T(8,128)(2,1)S(1)}, bf16[128,256]{1,0:T(8,128)(2,1)S(1)}, u32[]{:S(2)}, u32[]{:S(2)}) collective-permute-start(bf16[128,256]{1,0:T(8,128)(2,1)S(1)} %get-tuple-element.49), channel_id=1, source_target_pairs={{0,1},{1,2},{2,3},{3,0},{4,5},{5,6},{6,7},{7,4},{8,9},{9,10},{10,1... | collective-permute-start | bytes 196616 | tf_op jit(solution)/shard_map/ppermute | solution.py:345
  16.4 5.8 %collective-permute-start.4 = (bf16[128,256]{1,0:T(8,128)(2,1)S(1)}, bf16[128,256]{1,0:T(8,128)(2,1)S(1)}, u32[]{:S(2)}, u32[]{:S(2)}) collective-permute-start(bf16[128,256]{1,0:T(8,128)(2,1)S(1)} %get-tuple-element.49), channel_id=1, source_target_pairs={{0,2},{1,3},{2,0},{3,1},{4,6},{5,7},{6,4},{7,5},{8,10},{9,11},{10,... | collective-permute-start | bytes 196616 | tf_op jit(solution)/shard_map/ppermute | solution.py:345
  19.3 4.3 %collective-permute-start.5 = (bf16[128,256]{1,0:T(8,128)(2,1)S(1)}, bf16[128,256]{1,0:T(8,128)(2,1)S(1)}, u32[]{:S(2)}, u32[]{:S(2)}) collective-permute-start(bf16[128,256]{1,0:T(8,128)(2,1)S(1)} %get-tuple-element.49), channel_id=1, source_target_pairs={{0,3},{1,0},{2,1},{3,2},{4,7},{5,4},{6,5},{7,6},{8,11},{9,8},{10,9... | collective-permute-start | bytes 196616 | tf_op jit(solution)/shard_map/ppermute | solution.py:345
  23.6 9.4 %collective-permute-start.10 = (bf16[512,256]{1,0:T(8,128)(2,1)S(1)}, bf16[512,256]{1,0:T(8,128)(2,1)S(1)}, u32[]{:S(2)}, u32[]{:S(2)}) collective-permute-start(bf16[512,256]{1,0:T(8,128)(2,1)S(1)} %get-tuple-element.59.refs_4_), channel_id=1, source_target_pairs={{0,8},{1,9},{2,10},{3,11},{4,12},{5,13},{6,14},{7,15},{8,0},{9,1},... | collective-permute-start | bytes 786440 | tf_op jit(solution)/shard_map/ppermute | solution.py:345
  24.2 18.2 %collective-permute-start.11 = (bf16[512,256]{1,0:T(8,128)(2,1)S(1)}, bf16[512,256]{1,0:T(8,128)(2,1)S(1)}, u32[]{:S(2)}, u32[]{:S(2)}) collective-permute-start(bf16[512,256]{1,0:T(8,128)(2,1)S(1)} %get-tuple-element.59.refs_4_), channel_id=1, source_target_pairs={{0,12},{1,13},{2,14},{3,15},{4,0},{5,1},{6,2},{7,3},{8,4},{9,5},{1... | collective-permute-start | bytes 786440 | tf_op jit(solution)/shard_map/ppermute | solution.py:345
  27.0 15.4 %collective-permute-start.6 = (bf16[512,256]{1,0:T(8,128)(2,1)S(1)}, bf16[512,256]{1,0:T(8,128)(2,1)S(1)}, u32[]{:S(2)}, u32[]{:S(2)}) collective-permute-start(bf16[512,256]{1,0:T(8,128)(2,1)S(1)} %get-tuple-element.55.refs_0_), channel_id=1, source_target_pairs={{0,1},{1,2},{2,3},{3,0},{4,5},{5,6},{6,7},{7,4},{8,9},{9,10},{10,1... | collective-permute-start | bytes 786440 | tf_op jit(solution)/shard_map/ppermute | solution.py:345
  27.3 15.1 %collective-permute-start.7 = (bf16[512,256]{1,0:T(8,128)(2,1)S(1)}, bf16[512,256]{1,0:T(8,128)(2,1)S(1)}, u32[]{:S(2)}, u32[]{:S(2)}) collective-permute-start(bf16[512,256]{1,0:T(8,128)(2,1)S(1)} %get-tuple-element.55.refs_0_), channel_id=1, source_target_pairs={{0,2},{1,3},{2,0},{3,1},{4,6},{5,7},{6,4},{7,5},{8,10},{9,11},{10,... | collective-permute-start | bytes 786440 | tf_op jit(solution)/shard_map/ppermute | solution.py:345
  31.0 11.4 %collective-permute-start.8 = (bf16[512,256]{1,0:T(8,128)(2,1)S(1)}, bf16[512,256]{1,0:T(8,128)(2,1)S(1)}, u32[]{:S(2)}, u32[]{:S(2)}) collective-permute-start(bf16[512,256]{1,0:T(8,128)(2,1)S(1)} %get-tuple-element.55.refs_0_), channel_id=1, source_target_pairs={{0,3},{1,0},{2,1},{3,2},{4,7},{5,4},{6,5},{7,6},{8,11},{9,8},{10,9... | collective-permute-start | bytes 786440 | tf_op jit(solution)/shard_map/ppermute | solution.py:345
  33.0 9.4 %collective-permute-start.9 = (bf16[512,256]{1,0:T(8,128)(2,1)S(1)}, bf16[512,256]{1,0:T(8,128)(2,1)S(1)}, u32[]{:S(2)}, u32[]{:S(2)}) collective-permute-start(bf16[512,256]{1,0:T(8,128)(2,1)S(1)} %get-tuple-element.59.refs_4_), channel_id=1, source_target_pairs={{0,4},{1,5},{2,6},{3,7},{4,8},{5,9},{6,10},{7,11},{8,12},{9,13},{1... | collective-permute-start | bytes 786440 | tf_op jit(solution)/shard_map/ppermute | solution.py:345
  55.5 35.5 %all-to-all-start.1 = ((bf16[16,528,128]{2,1,0:T(8,128)(2,1)}), bf16[16,528,128]{2,1,0:T(8,128)(2,1)S(1)}, u32[]{:S(2)}, u32[]{:S(2)}) async-start(bf16[16,528,128]{2,1,0:T(8,128)(2,1)} %attend.3), calls=%async_computation.1 | async-start | bytes 4325376 | tf_op jit(solution)/shard_map/all_to_all | solution.py:324
  92.3 32.5 %all-to-all-start = ((bf16[16,528,128]{2,1,0:T(8,128)(2,1)}), bf16[16,528,128]{2,1,0:T(8,128)(2,1)S(1)}, u32[]{:S(2)}, u32[]{:S(2)}) async-start(bf16[16,528,128]{2,1,0:T(8,128)(2,1)} %attend.2), calls=%async_computation | async-start | bytes 4325376 | tf_op jit(solution)/shard_map/all_to_all | solution.py:324
  96.1 1.6 %copy-start.1 = (bf16[16,528,128]{2,1,0:T(8,128)(2,1)S(1)}, bf16[16,528,128]{2,1,0:T(8,128)(2,1)}, u32[]{:S(2)}) copy-start(bf16[16,528,128]{2,1,0:T(8,128)(2,1)} %copy-done) | copy-start | bytes 6488068
  101.7 2.2 %collective-permute-start.12 = (bf16[4,128,512]{2,1,0:T(8,128)(2,1)}, bf16[4,128,512]{2,1,0:T(8,128)(2,1)S(1)}, u32[]{:S(2)}, u32[]{:S(2)}) collective-permute-start(bf16[4,128,512]{2,1,0:T(8,128)(2,1)} %get-tuple-element.64), channel_id=1, source_target_pairs={{0,16},{16,0},{32,48},{48,32},{64,80},{80,64},{96,112},{112,96},{1... | collective-permute-start | bytes 1572872 | tf_op jit(solution)/shard_map/ppermute | solution.py:329
  104.0 6.8 %collective-permute-start.13 = (bf16[128,512]{1,0:T(8,128)(2,1)S(1)}, bf16[128,512]{1,0:T(8,128)(2,1)S(1)}, u32[]{:S(2)}, u32[]{:S(2)}) collective-permute-start(bf16[128,512]{1,0:T(8,128)(2,1)S(1)} %get-tuple-element.66), channel_id=1, source_target_pairs={{0,32},{16,48},{32,64},{48,80},{64,96},{80,112},{96,0},{112,16},{1... | collective-permute-start | bytes 393224 | tf_op jit(solution)/shard_map/ppermute | solution.py:333
  104.1 8.8 %collective-permute-start.14 = (bf16[128,512]{1,0:T(8,128)(2,1)S(1)}, bf16[128,512]{1,0:T(8,128)(2,1)S(1)}, u32[]{:S(2)}, u32[]{:S(2)}) collective-permute-start(bf16[128,512]{1,0:T(8,128)(2,1)S(1)} %get-tuple-element.67), channel_id=1, source_target_pairs={{0,96},{16,112},{32,0},{48,16},{64,32},{80,48},{96,64},{112,80},{1... | collective-permute-start | bytes 393224 | tf_op jit(solution)/shard_map/ppermute | solution.py:333
  107.3 6.5 %collective-permute-start.15 = (bf16[128,512]{1,0:T(8,128)(2,1)S(1)}, bf16[128,512]{1,0:T(8,128)(2,1)S(1)}, u32[]{:S(2)}, u32[]{:S(2)}) collective-permute-start(bf16[128,512]{1,0:T(8,128)(2,1)S(1)} %get-tuple-element.68), channel_id=1, source_target_pairs={{0,64},{16,80},{32,96},{48,112},{64,0},{80,16},{96,32},{112,48},{1... | collective-permute-start | bytes 393224 | tf_op jit(solution)/shard_map/ppermute | solution.py:333
  128.0 2.0 %collective-permute-start.16 = (bf16[4,128,512]{2,1,0:T(8,128)(2,1)S(1)}, bf16[4,128,512]{2,1,0:T(8,128)(2,1)S(1)}, u32[]{:S(2)}, u32[]{:S(2)}) collective-permute-start(bf16[4,128,512]{2,1,0:T(8,128)(2,1)S(1)} %get-tuple-element.72), channel_id=1, source_target_pairs={{0,16},{16,0},{32,48},{48,32},{64,80},{80,64},{96,112},{112,96},{1... | collective-permute-start | bytes 1572872 | tf_op jit(solution)/shard_map/ppermute | solution.py:329
  130.1 6.8 %collective-permute-start.17 = (bf16[128,512]{1,0:T(8,128)(2,1)S(1)}, bf16[128,512]{1,0:T(8,128)(2,1)S(1)}, u32[]{:S(2)}, u32[]{:S(2)}) collective-permute-start(bf16[128,512]{1,0:T(8,128)(2,1)S(1)} %get-tuple-element.74), channel_id=1, source_target_pairs={{0,32},{16,48},{32,64},{48,80},{64,96},{80,112},{96,0},{112,16},{1... | collective-permute-start | bytes 393224 | tf_op jit(solution)/shard_map/ppermute | solution.py:333
  130.2 8.0 %collective-permute-start.18 = (bf16[128,512]{1,0:T(8,128)(2,1)S(1)}, bf16[128,512]{1,0:T(8,128)(2,1)S(1)}, u32[]{:S(2)}, u32[]{:S(2)}) collective-permute-start(bf16[128,512]{1,0:T(8,128)(2,1)S(1)} %get-tuple-element.75), channel_id=1, source_target_pairs={{0,96},{16,112},{32,0},{48,16},{64,32},{80,48},{96,64},{112,80},{1... | collective-permute-start | bytes 393224 | tf_op jit(solution)/shard_map/ppermute | solution.py:333
  133.4 7.3 %collective-permute-start.19 = (bf16[128,512]{1,0:T(8,128)(2,1)S(1)}, bf16[128,512]{1,0:T(8,128)(2,1)S(1)}, u32[]{:S(2)}, u32[]{:S(2)}) collective-permute-start(bf16[128,512]{1,0:T(8,128)(2,1)S(1)} %get-tuple-element.76), channel_id=1, source_target_pairs={{0,64},{16,80},{32,96},{48,112},{64,0},{80,16},{96,32},{112,48},{1... | collective-permute-start | bytes 393224 | tf_op jit(solution)/shard_map/ppermute | solution.py:333
  (1 other events, 1.3 us)
Sparse Core Ops, SparseCore 0:
  9.5 50.9 all-gather.1

commit v3 on v2

--- a/solution.py
+++ b/solution.py
@@ -63,8 +63,7 @@
     dx = (me // side - owner // side) % side
     dy = (me % side - owner % side) % side
     head = jnp.arange(heads, dtype=jnp.int32)[:, None]
-    near = jnp.where(head < heads // 2, dy * side + dx, dx * side + dy)
-    position = jnp.where(chunk == 0, near, owner)
+    position = jnp.where(head < heads // 2, dy * side + dx, dx * side + dy)
     codes = (((chunk * 16 + head) * 256 + owner) * 256 + position) * 256 + tile
     smem = pl.BlockSpec(memory_space=pltpu.SMEM)
     return pl.pallas_call(
@@ -78,6 +77,29 @@
         compiler_params=pltpu.CompilerParams(vmem_limit_bytes=1024 * 1024),
         name="plan",
     )(codes, counts)
+
+
+def regroup_kernel(side, *refs):
+    pieces, lines = refs[: 2 * side], refs[2 * side :]
+    for n, line in enumerate(lines):
+        chunk, half = divmod(n, 2)
+        for d in range(side):
+            piece = pieces[half * side + d]
+            line[d * BLOCK : (d + 1) * BLOCK] = piece[chunk * BLOCK : (chunk + 1) * BLOCK]
+
+
+def regroup(halves, side, owned):
+    vmem = pl.BlockSpec(memory_space=pltpu.VMEM)
+    line = jax.ShapeDtypeStruct((side * BLOCK, halves[0].shape[1]), BF16)
+    lines = pl.pallas_call(
+        functools.partial(regroup_kernel, side),
+        out_shape=[line] * (2 * owned),
+        in_specs=[vmem] * (2 * side),
+        out_specs=[vmem] * (2 * owned),
+        compiler_params=pltpu.CompilerParams(vmem_limit_bytes=8 * 1024 * 1024),
+        name="regroup",
+    )(*halves)
+    return [(lines[2 * c], lines[2 * c + 1]) for c in range(owned)]
 
 
 def attend_kernel(chunk, sources, entries, starts, *refs):
@@ -220,7 +242,7 @@
             pltpu.VMEM((3 * heads, owners, BLOCK), F32),
             pltpu.SemaphoreType.DMA((heads, 2 + max(len(p) for p in sources))),
         ],
-        compiler_params=pltpu.CompilerParams(vmem_limit_bytes=40 * 1024 * 1024),
+        compiler_params=pltpu.CompilerParams(vmem_limit_bytes=28 * 1024 * 1024),
         name="attend",
     )(entries, starts, *queries, in_hbm(keys), in_hbm(values))
 
@@ -278,7 +300,7 @@
                 pltpu.SemaphoreType.DMA((zs, 2)),
             ],
         ),
-        compiler_params=pltpu.CompilerParams(vmem_limit_bytes=24 * 1024 * 1024),
+        compiler_params=pltpu.CompilerParams(vmem_limit_bytes=14 * 1024 * 1024),
         name="project",
     )(core, parts, in_hbm(weight))
 
@@ -333,9 +355,6 @@
             total = total + lax.ppermute(piece, "heads", pairs).astype(F32)
         return total.astype(BF16)
 
-    def rows(c):
-        return queries[c * BLOCK : (c + 1) * BLOCK]
-
     def along(x, axis):
         def pairs(d):
             there = lambda i, j: ((i + d) % side, j) if axis == 0 else (i, (j + d) % side)
@@ -345,28 +364,24 @@
         got = {d: lax.ppermute(x, "keys", pairs(d)) for d in Z_STEPS}
         return [x] + [got[d] for d in range(1, side)]
 
-    near = rows(0)
-    middle = near.shape[1] // 2
-    left, right = near[:, :middle], near[:, middle:]
+    middle = queries.shape[1] // 2
+    left, right = queries[:, :middle], queries[:, middle:]
     left, right = lax.optimization_barrier((left, right))
-    halves = along(left, 0) + along(right, 1)
-    halves = lax.optimization_barrier(halves)
-    left, right = jnp.concatenate(halves[:side]), jnp.concatenate(halves[side:])
-    left, right = lax.optimization_barrier((left, right))
-    direct = lax.optimization_barrier(along(left, 1) + along(right, 0))
+    halves = lax.optimization_barrier(along(left, 0) + along(right, 1))
+
+    sources = []
+    for left, right in regroup(halves, side, owned):
+        sources.append(lax.optimization_barrier(along(left, 1) + along(right, 0)))
     lower = [[(i, h) for i in range(side)] for h in range(heads // 2)]
     upper = [[(side + i, h) for i in range(side)] for h in range(heads // 2)]
-    whole = [[(0, h)] for h in range(heads)]
 
     slot = jnp.reshape(lax.axis_index("keys"), (1,)).astype(jnp.int32)
     entries, starts = plan(slot, block_ids, block_counts, tiles, owned, side)
     outs = []
     for c in range(owned):
-        if c == 0:
-            source, lanes = direct, lower + upper
-        else:
-            source, lanes = [in_hbm(lax.all_gather(rows(c), "keys", axis=0, tiled=True))], whole
-        parts = attend(c, entries, starts, source, lanes, key_states, value_states)
+        parts = attend(
+            c, entries, starts, sources[c], lower + upper, key_states, value_states
+        )
         got = exchange(parts)
         if outs:
             got, outs[-1] = lax.optimization_barrier((got, outs[-1]))

time: 150 us -> 160 us (1.067); the launches traced: 148 us -> 163 us
  starting transfers between devices: 40.4 us -> 67.5 us
  between operations: 13.6 us -> 0.2 us
    ppermute x12 -> x18, waiting for transfers between devices: 4.82 us -> 34.6 us  [along(): got = {d: lax.ppermute(x, 'keys', pairs(d)) for d in Z_STEPS}]
    all_to_all x2, waiting for transfers between devices: 28.8 us -> 0.01 us  [exchange(): lax.all_to_all(parts, 'keys', split_axis=0, concat_axis=0, tiled=True)]
    ppermute x6, starting transfers between devices: 10.1 us -> 24.2 us  [finish(): total = total + lax.ppermute(piece, 'heads', pairs).astype(F32)]
    ppermute x12 -> x18, starting transfers between devices: 22.4 us -> 33.1 us  [along(): got = {d: lax.ppermute(x, 'keys', pairs(d)) for d in Z_STEPS}]
    all_to_all x2, starting transfers between devices: 7.72 us -> 10 us  [exchange(): lax.all_to_all(parts, 'keys', split_axis=0, concat_axis=0, tiled=True)]
  transfers between devices with their start and end apart: 23 -> 28, of which waited for: 15 -> 16; matrix products, arithmetic and copies ran while one was open for 2% -> 1% of each run, Pallas kernels for 23% -> 14%
where the time goes in v3:
time: 160 us; the launch traced here: 163 us
  starting transfers between devices  67.5 us (42%)
  waiting for transfers between devices  49.5 us (31%)
  Pallas kernels  39.3 us (25%)
  local copies, waits for them, and re-layouts  4.67 us (3%)
  other arithmetic  1.62 us (1%)
    ppermute x18, waiting for transfers between devices, along(): got = {d: lax.ppermute(x, 'keys', pairs(d)) for d in Z_STEPS}  34.6 us
    ppermute x18, starting transfers between devices, along(): got = {d: lax.ppermute(x, 'keys', pairs(d)) for d in Z_STEPS}  33.1 us
    pallas_call x2, Pallas kernels, attend(): pl.pallas_call(functools.partial(attend_kernel, chunk, sources), out_shap...  27 us
    ppermute x6, starting transfers between devices, finish(): total = total + lax.ppermute(piece, 'heads', pairs).astype(F32)  24.2 us
    ppermute x6, waiting for transfers between devices, finish(): total = total + lax.ppermute(piece, 'heads', pairs).astype(F32)  10.9 us
    all_to_all x2, starting transfers between devices, exchange(): lax.all_to_all(parts, 'keys', split_axis=0, concat_axis=0, tiled=True)  10 us
    pallas_call x2, Pallas kernels, project(): pl.pallas_call(functools.partial(project_kernel, heads), out_shape=[jax.S...  7.14 us
    pallas_call x1, Pallas kernels, plan(): pl.pallas_call(functools.partial(plan_kernel, owned), out_shape=(jax.Shap...  4.89 us
  transfers between devices with their start and end apart: 28, of which 16 were waited for; matrix products, arithmetic and copies ran while one was open for 1% of the time, Pallas kernels for 14%

profile of v3, /device:TPU:0, one launch (start us, length us, event | category | flops | bytes accessed | tf_op | source)
XLA Modules:
  0.0 162.8 jit_solution(16783310150279455301)
XLA Ops:
  2.6 2.7 %collective-permute-start.1 = (bf16[256,256]{1,0:T(8,128)(2,1)S(1)}, bf16[256,256]{1,0:T(8,128)(2,1)S(1)}, u32[]{:S(2)}, u32[]{:S(2)}) collective-permute-start(bf16[256,256]{1,0:T(8,128)(2,1)S(1)} %get-tuple-element.55.refs_0_), channel_id=1, source_target_pairs={{0,8},{1,9},{2,10},{3,11},{4,12},{5,13},{6,14},{7,15},{8,0},{9,1},... | collective-permute-start | bytes 393224 | tf_op jit(solution)/shard_map/ppermute | solution.py:364
  8.4 2.9 %collective-permute-start.4 = (bf16[256,256]{1,0:T(8,128)(2,1)S(1)}, bf16[256,256]{1,0:T(8,128)(2,1)S(1)}, u32[]{:S(2)}, u32[]{:S(2)}) collective-permute-start(bf16[256,256]{1,0:T(8,128)(2,1)S(1)} %get-tuple-element.59.refs_4_), channel_id=1, source_target_pairs={{0,2},{1,3},{2,0},{3,1},{4,6},{5,7},{6,4},{7,5},{8,10},{9,11},{10,... | collective-permute-start | bytes 393224 | tf_op jit(solution)/shard_map/ppermute | solution.py:364
  14.3 2.1 %collective-permute-done.4.refs_6_ = bf16[256,256]{1,0:T(8,128)(2,1)S(1)} collective-permute-done((bf16[256,256]{1,0:T(8,128)(2,1)S(1)}, bf16[256,256]{1,0:T(8,128)(2,1)S(1)}, u32[]{:S(2)}, u32[]{:S(2)}) %collective-permute-start.4) | collective-permute-done | bytes 131104 | tf_op jit(solution)/shard_map/ppermute | solution.py:364
  17.7 2.9 %collective-permute-start.13 = (bf16[512,256]{1,0:T(8,128)(2,1)S(1)}, bf16[512,256]{1,0:T(8,128)(2,1)S(1)}, u32[]{:S(2)}, u32[]{:S(2)}) collective-permute-start(bf16[512,256]{1,0:T(8,128)(2,1)S(1)} %get-tuple-element.75.refs_0_), channel_id=1, source_target_pairs={{0,2},{1,3},{2,0},{3,1},{4,6},{5,7},{6,4},{7,5},{8,10},{9,11},{10,... | collective-permute-start | bytes 786440 | tf_op jit(solution)/shard_map/ppermute | solution.py:364
  23.6 2.4 %collective-permute-done.12.refs_1_ = bf16[512,256]{1,0:T(8,128)(2,1)S(1)} collective-permute-done((bf16[512,256]{1,0:T(8,128)(2,1)S(1)}, bf16[512,256]{1,0:T(8,128)(2,1)S(1)}, u32[]{:S(2)}, u32[]{:S(2)}) %collective-permute-start.12) | collective-permute-done | bytes 262176 | tf_op jit(solution)/shard_map/ppermute | solution.py:364
  28.6 4.9 %plan.1 = (s32[2,776]{1,0:T(2,128)S(1)}, s32[2,5]{1,0:T(2,128)S(1)}) custom-call(s32[4,192]{1,0:T(4,128)S(1)} %fusion.7.codes, s32[4,1]{1,0:T(4,128)S(1)} %copy.7.counts), custom_call_target="tpu_custom_call" | custom-call | tf_op jit(solution)/shard_map/plan/pallas_call | solution.py:69
  34.5 13.1 %attend.3 = bf16[16,528,128]{2,1,0:T(8,128)(2,1)} custom-call(s32[2,776]{1,0:T(2,128)S(1)} %get-tuple-element.51.entries, s32[2,5]{1,0:T(2,128)S(1)} %get-tuple-element.52.starts, bf16[512,256]{1,0:T(8,128)(2,1)S(1)} %get-tuple-element.75.refs_0_, bf16[512,256]{1,0:T(8,128)(2,1)S(1)} %collective-permute-done.12.refs_1_, ...), custom_call_target="tpu_custom_call" | custom-call | tf_op jit(solution)/shard_map/attend/pallas_call | solution.py:231
  47.6 5.5 %all-to-all-start.1 = ((bf16[16,528,128]{2,1,0:T(8,128)(2,1)}), bf16[16,528,128]{2,1,0:T(8,128)(2,1)S(1)}, u32[]{:S(2)}, u32[]{:S(2)}) async-start(bf16[16,528,128]{2,1,0:T(8,128)(2,1)} %attend.3), calls=%async_computation.1 | async-start | bytes 4325376 | tf_op jit(solution)/shard_map/all_to_all | solution.py:346
  53.1 3.4 %collective-permute-start.10 = (bf16[512,256]{1,0:T(8,128)(2,1)S(1)}, bf16[512,256]{1,0:T(8,128)(2,1)S(1)}, u32[]{:S(2)}, u32[]{:S(2)}) collective-permute-start(bf16[512,256]{1,0:T(8,128)(2,1)S(1)} %get-tuple-element.69.refs_4_), channel_id=1, source_target_pairs={{0,8},{1,9},{2,10},{3,11},{4,12},{5,13},{6,14},{7,15},{8,0},{9,1},... | collective-permute-start | bytes 786440 | tf_op jit(solution)/shard_map/ppermute | solution.py:364
  59.1 2.7 %collective-permute-start.7 = (bf16[512,256]{1,0:T(8,128)(2,1)S(1)}, bf16[512,256]{1,0:T(8,128)(2,1)S(1)}, u32[]{:S(2)}, u32[]{:S(2)}) collective-permute-start(bf16[512,256]{1,0:T(8,128)(2,1)S(1)} %get-tuple-element.65.refs_0_), channel_id=1, source_target_pairs={{0,2},{1,3},{2,0},{3,1},{4,6},{5,7},{6,4},{7,5},{8,10},{9,11},{10,... | collective-permute-start | bytes 786440 | tf_op jit(solution)/shard_map/ppermute | solution.py:364
  63.3 22.9 %collective-permute-done.10.refs_6_ = bf16[512,256]{1,0:T(8,128)(2,1)S(1)} collective-permute-done((bf16[512,256]{1,0:T(8,128)(2,1)S(1)}, bf16[512,256]{1,0:T(8,128)(2,1)S(1)}, u32[]{:S(2)}, u32[]{:S(2)}) %collective-permute-start.10) | collective-permute-done | bytes 262176 | tf_op jit(solution)/shard_map/ppermute | solution.py:364
  86.2 3.2 %collective-permute-start.9 = (bf16[512,256]{1,0:T(8,128)(2,1)S(1)}, bf16[512,256]{1,0:T(8,128)(2,1)S(1)}, u32[]{:S(2)}, u32[]{:S(2)}) collective-permute-start(bf16[512,256]{1,0:T(8,128)(2,1)S(1)} %get-tuple-element.69.refs_4_), channel_id=1, source_target_pairs={{0,4},{1,5},{2,6},{3,7},{4,8},{5,9},{6,10},{7,11},{8,12},{9,13},{1... | collective-permute-start | bytes 786440 | tf_op jit(solution)/shard_map/ppermute | solution.py:364
  89.4 4.4 %collective-permute-done.9.refs_5_ = bf16[512,256]{1,0:T(8,128)(2,1)S(1)} collective-permute-done((bf16[512,256]{1,0:T(8,128)(2,1)S(1)}, bf16[512,256]{1,0:T(8,128)(2,1)S(1)}, u32[]{:S(2)}, u32[]{:S(2)}) %collective-permute-start.9) | collective-permute-done | bytes 262176 | tf_op jit(solution)/shard_map/ppermute | solution.py:364
  93.8 13.9 %attend.2 = bf16[16,528,128]{2,1,0:T(8,128)(2,1)} custom-call(s32[2,776]{1,0:T(2,128)S(1)} %get-tuple-element.51.entries, s32[2,5]{1,0:T(2,128)S(1)} %get-tuple-element.52.starts, bf16[512,256]{1,0:T(8,128)(2,1)S(1)} %get-tuple-element.65.refs_0_, bf16[512,256]{1,0:T(8,128)(2,1)S(1)} %collective-permute-done.6.refs_1_, ...), custom_call_target="tpu_custom_call" | custom-call | tf_op jit(solution)/shard_map/attend/pallas_call | solution.py:231
  109.0 4.5 %all-to-all-start = ((bf16[16,528,128]{2,1,0:T(8,128)(2,1)}), bf16[16,528,128]{2,1,0:T(8,128)(2,1)S(1)}, u32[]{:S(2)}, u32[]{:S(2)}) async-start(bf16[16,528,128]{2,1,0:T(8,128)(2,1)} %attend.2), calls=%async_computation | async-start | bytes 4325376 | tf_op jit(solution)/shard_map/all_to_all | solution.py:346
  115.2 4.0 %project.2 = (bf16[4,128,512]{2,1,0:T(8,128)(2,1)S(1)}, bf16[4,128,512]{2,1,0:T(8,128)(2,1)}) custom-call(s32[1]{0:T(128)} %bitcast.4.core, bf16[16,528,128]{2,1,0:T(8,128)(2,1)S(1)} %copy-done.1, bf16[512,4096]{1,0:T(8,128)(2,1)} %weight.3), custom_call_target="tpu_custom_call" | custom-call | tf_op jit(solution)/shard_map/project/pallas_call | solution.py:286
  121.5 5.2 %collective-permute-start.19 = (bf16[128,512]{1,0:T(8,128)(2,1)S(1)}, bf16[128,512]{1,0:T(8,128)(2,1)S(1)}, u32[]{:S(2)}, u32[]{:S(2)}) collective-permute-start(bf16[128,512]{1,0:T(8,128)(2,1)S(1)} %get-tuple-element.86), channel_id=1, source_target_pairs={{0,32},{16,48},{32,64},{48,80},{64,96},{80,112},{96,0},{112,16},{1... | collective-permute-start | bytes 393224 | tf_op jit(solution)/shard_map/ppermute | solution.py:355
  126.7 3.9 %collective-permute-start.20 = (bf16[128,512]{1,0:T(8,128)(2,1)S(1)}, bf16[128,512]{1,0:T(8,128)(2,1)S(1)}, u32[]{:S(2)}, u32[]{:S(2)}) collective-permute-start(bf16[128,512]{1,0:T(8,128)(2,1)S(1)} %get-tuple-element.87), channel_id=1, source_target_pairs={{0,96},{16,112},{32,0},{48,16},{64,32},{80,48},{96,64},{112,80},{1... | collective-permute-start | bytes 393224 | tf_op jit(solution)/shard_map/ppermute | solution.py:355
  132.0 2.3 %collective-permute-done.19 = bf16[128,512]{1,0:T(8,128)(2,1)S(1)} collective-permute-done((bf16[128,512]{1,0:T(8,128)(2,1)S(1)}, bf16[128,512]{1,0:T(8,128)(2,1)S(1)}, u32[]{:S(2)}, u32[]{:S(2)}) %collective-permute-start.19) | collective-permute-done | bytes 131104 | tf_op jit(solution)/shard_map/ppermute | solution.py:355
  134.3 2.2 %collective-permute-done.20 = bf16[128,512]{1,0:T(8,128)(2,1)S(1)} collective-permute-done((bf16[128,512]{1,0:T(8,128)(2,1)S(1)}, bf16[128,512]{1,0:T(8,128)(2,1)S(1)}, u32[]{:S(2)}, u32[]{:S(2)}) %collective-permute-start.20) | collective-permute-done | bytes 131104 | tf_op jit(solution)/shard_map/ppermute | solution.py:355
  138.4 3.2 %project.3 = (bf16[4,128,512]{2,1,0:T(8,128)(2,1)S(1)}, bf16[4,128,512]{2,1,0:T(8,128)(2,1)S(1)}) custom-call(s32[1]{0:T(128)} %bitcast.4.core, bf16[16,528,128]{2,1,0:T(8,128)(2,1)S(1)} %all-to-all-done.in_ref, bf16[512,4096]{1,0:T(8,128)(2,1)} %weight.3), custom_call_target="tpu_custom_call" | custom-call | tf_op jit(solution)/shard_map/project/pallas_call | solution.py:286
  143.7 11.6 %collective-permute-start.23 = (bf16[128,512]{1,0:T(8,128)(2,1)S(1)}, bf16[128,512]{1,0:T(8,128)(2,1)S(1)}, u32[]{:S(2)}, u32[]{:S(2)}) collective-permute-start(bf16[128,512]{1,0:T(8,128)(2,1)S(1)} %get-tuple-element.94), channel_id=1, source_target_pairs={{0,32},{16,48},{32,64},{48,80},{64,96},{80,112},{96,0},{112,16},{1... | collective-permute-start | bytes 393224 | tf_op jit(solution)/shard_map/ppermute | solution.py:355
  155.3 2.1 %collective-permute-start.25 = (bf16[128,512]{1,0:T(8,128)(2,1)S(1)}, bf16[128,512]{1,0:T(8,128)(2,1)S(1)}, u32[]{:S(2)}, u32[]{:S(2)}) collective-permute-start(bf16[128,512]{1,0:T(8,128)(2,1)S(1)} %get-tuple-element.96), channel_id=1, source_target_pairs={{0,64},{16,80},{32,96},{48,112},{64,0},{80,16},{96,32},{112,48},{1... | collective-permute-start | bytes 393224 | tf_op jit(solution)/shard_map/ppermute | solution.py:355
  159.1 2.5 %collective-permute-done.24 = bf16[128,512]{1,0:T(8,128)(2,1)S(1)} collective-permute-done((bf16[128,512]{1,0:T(8,128)(2,1)S(1)}, bf16[128,512]{1,0:T(8,128)(2,1)S(1)}, u32[]{:S(2)}, u32[]{:S(2)}) %collective-permute-start.24) | collective-permute-done | bytes 131104 | tf_op jit(solution)/shard_map/ppermute | solution.py:355
  (51 shorter events, 34.0 us)
Async XLA Ops:
  1.0 10.3 %collective-permute-start = (bf16[256,256]{1,0:T(8,128)(2,1)S(1)}, bf16[256,256]{1,0:T(8,128)(2,1)S(1)}, u32[]{:S(2)}, u32[]{:S(2)}) collective-permute-start(bf16[256,256]{1,0:T(8,128)(2,1)S(1)} %get-tuple-element.55.refs_0_), channel_id=1, source_target_pairs={{0,4},{1,5},{2,6},{3,7},{4,8},{5,9},{6,10},{7,11},{8,12},{9,13},{1... | collective-permute-start | bytes 393224 | tf_op jit(solution)/shard_map/ppermute | solution.py:364
  2.6 10.0 %collective-permute-start.1 = (bf16[256,256]{1,0:T(8,128)(2,1)S(1)}, bf16[256,256]{1,0:T(8,128)(2,1)S(1)}, u32[]{:S(2)}, u32[]{:S(2)}) collective-permute-start(bf16[256,256]{1,0:T(8,128)(2,1)S(1)} %get-tuple-element.55.refs_0_), channel_id=1, source_target_pairs={{0,8},{1,9},{2,10},{3,11},{4,12},{5,13},{6,14},{7,15},{8,0},{9,1},... | collective-permute-start | bytes 393224 | tf_op jit(solution)/shard_map/ppermute | solution.py:364
  5.4 7.3 %collective-permute-start.2 = (bf16[256,256]{1,0:T(8,128)(2,1)S(1)}, bf16[256,256]{1,0:T(8,128)(2,1)S(1)}, u32[]{:S(2)}, u32[]{:S(2)}) collective-permute-start(bf16[256,256]{1,0:T(8,128)(2,1)S(1)} %get-tuple-element.55.refs_0_), channel_id=1, source_target_pairs={{0,12},{1,13},{2,14},{3,15},{4,0},{5,1},{6,2},{7,3},{8,4},{9,5},{1... | collective-permute-start | bytes 393224 | tf_op jit(solution)/shard_map/ppermute | solution.py:364
  6.8 7.5 %collective-permute-start.3 = (bf16[256,256]{1,0:T(8,128)(2,1)S(1)}, bf16[256,256]{1,0:T(8,128)(2,1)S(1)}, u32[]{:S(2)}, u32[]{:S(2)}) collective-permute-start(bf16[256,256]{1,0:T(8,128)(2,1)S(1)} %get-tuple-element.59.refs_4_), channel_id=1, source_target_pairs={{0,1},{1,2},{2,3},{3,0},{4,5},{5,6},{6,7},{7,4},{8,9},{9,10},{10,1... | collective-permute-start | bytes 393224 | tf_op jit(solution)/shard_map/ppermute | solution.py:364
  8.4 8.1 %collective-permute-start.4 = (bf16[256,256]{1,0:T(8,128)(2,1)S(1)}, bf16[256,256]{1,0:T(8,128)(2,1)S(1)}, u32[]{:S(2)}, u32[]{:S(2)}) collective-permute-start(bf16[256,256]{1,0:T(8,128)(2,1)S(1)} %get-tuple-element.59.refs_4_), channel_id=1, source_target_pairs={{0,2},{1,3},{2,0},{3,1},{4,6},{5,7},{6,4},{7,5},{8,10},{9,11},{10,... | collective-permute-start | bytes 393224 | tf_op jit(solution)/shard_map/ppermute | solution.py:364
  16.6 9.4 %collective-permute-start.12 = (bf16[512,256]{1,0:T(8,128)(2,1)S(1)}, bf16[512,256]{1,0:T(8,128)(2,1)S(1)}, u32[]{:S(2)}, u32[]{:S(2)}) collective-permute-start(bf16[512,256]{1,0:T(8,128)(2,1)S(1)} %get-tuple-element.75.refs_0_), channel_id=1, source_target_pairs={{0,1},{1,2},{2,3},{3,0},{4,5},{5,6},{6,7},{7,4},{8,9},{9,10},{10,1... | collective-permute-start | bytes 786440 | tf_op jit(solution)/shard_map/ppermute | solution.py:364
  17.7 15.8 %collective-permute-start.13 = (bf16[512,256]{1,0:T(8,128)(2,1)S(1)}, bf16[512,256]{1,0:T(8,128)(2,1)S(1)}, u32[]{:S(2)}, u32[]{:S(2)}) collective-permute-start(bf16[512,256]{1,0:T(8,128)(2,1)S(1)} %get-tuple-element.75.refs_0_), channel_id=1, source_target_pairs={{0,2},{1,3},{2,0},{3,1},{4,6},{5,7},{6,4},{7,5},{8,10},{9,11},{10,... | collective-permute-start | bytes 786440 | tf_op jit(solution)/shard_map/ppermute | solution.py:364
  20.7 12.9 %collective-permute-start.14 = (bf16[512,256]{1,0:T(8,128)(2,1)S(1)}, bf16[512,256]{1,0:T(8,128)(2,1)S(1)}, u32[]{:S(2)}, u32[]{:S(2)}) collective-permute-start(bf16[512,256]{1,0:T(8,128)(2,1)S(1)} %get-tuple-element.75.refs_0_), channel_id=1, source_target_pairs={{0,3},{1,0},{2,1},{3,2},{4,7},{5,4},{6,5},{7,6},{8,11},{9,8},{10,9... | collective-permute-start | bytes 786440 | tf_op jit(solution)/shard_map/ppermute | solution.py:364
  21.8 12.0 %collective-permute-start.15 = (bf16[512,256]{1,0:T(8,128)(2,1)S(1)}, bf16[512,256]{1,0:T(8,128)(2,1)S(1)}, u32[]{:S(2)}, u32[]{:S(2)}) collective-permute-start(bf16[512,256]{1,0:T(8,128)(2,1)S(1)} %get-tuple-element.79.refs_4_), channel_id=1, source_target_pairs={{0,4},{1,5},{2,6},{3,7},{4,8},{5,9},{6,10},{7,11},{8,12},{9,13},{1... | collective-permute-start | bytes 786440 | tf_op jit(solution)/shard_map/ppermute | solution.py:364
  22.4 11.4 %collective-permute-start.16 = (bf16[512,256]{1,0:T(8,128)(2,1)S(1)}, bf16[512,256]{1,0:T(8,128)(2,1)S(1)}, u32[]{:S(2)}, u32[]{:S(2)}) collective-permute-start(bf16[512,256]{1,0:T(8,128)(2,1)S(1)} %get-tuple-element.79.refs_4_), channel_id=1, source_target_pairs={{0,8},{1,9},{2,10},{3,11},{4,12},{5,13},{6,14},{7,15},{8,0},{9,1},... | collective-permute-start | bytes 786440 | tf_op jit(solution)/shard_map/ppermute | solution.py:364
  26.0 8.5 %collective-permute-start.17 = (bf16[512,256]{1,0:T(8,128)(2,1)S(1)}, bf16[512,256]{1,0:T(8,128)(2,1)S(1)}, u32[]{:S(2)}, u32[]{:S(2)}) collective-permute-start(bf16[512,256]{1,0:T(8,128)(2,1)S(1)} %get-tuple-element.79.refs_4_), channel_id=1, source_target_pairs={{0,12},{1,13},{2,14},{3,15},{4,0},{5,1},{6,2},{7,3},{8,4},{9,5},{1... | collective-permute-start | bytes 786440 | tf_op jit(solution)/shard_map/ppermute | solution.py:364
  47.6 60.0 %all-to-all-start.1 = ((bf16[16,528,128]{2,1,0:T(8,128)(2,1)}), bf16[16,528,128]{2,1,0:T(8,128)(2,1)S(1)}, u32[]{:S(2)}, u32[]{:S(2)}) async-start(bf16[16,528,128]{2,1,0:T(8,128)(2,1)} %attend.3), calls=%async_computation.1 | async-start | bytes 4325376 | tf_op jit(solution)/shard_map/all_to_all | solution.py:346
  53.1 33.1 %collective-permute-start.10 = (bf16[512,256]{1,0:T(8,128)(2,1)S(1)}, bf16[512,256]{1,0:T(8,128)(2,1)S(1)}, u32[]{:S(2)}, u32[]{:S(2)}) collective-permute-start(bf16[512,256]{1,0:T(8,128)(2,1)S(1)} %get-tuple-element.69.refs_4_), channel_id=1, source_target_pairs={{0,8},{1,9},{2,10},{3,11},{4,12},{5,13},{6,14},{7,15},{8,0},{9,1},... | collective-permute-start | bytes 786440 | tf_op jit(solution)/shard_map/ppermute | solution.py:364
  56.5 32.9 %collective-permute-start.11 = (bf16[512,256]{1,0:T(8,128)(2,1)S(1)}, bf16[512,256]{1,0:T(8,128)(2,1)S(1)}, u32[]{:S(2)}, u32[]{:S(2)}) collective-permute-start(bf16[512,256]{1,0:T(8,128)(2,1)S(1)} %get-tuple-element.69.refs_4_), channel_id=1, source_target_pairs={{0,12},{1,13},{2,14},{3,15},{4,0},{5,1},{6,2},{7,3},{8,4},{9,5},{1... | collective-permute-start | bytes 786440 | tf_op jit(solution)/shard_map/ppermute | solution.py:364
  57.7 31.7 %collective-permute-start.6 = (bf16[512,256]{1,0:T(8,128)(2,1)S(1)}, bf16[512,256]{1,0:T(8,128)(2,1)S(1)}, u32[]{:S(2)}, u32[]{:S(2)}) collective-permute-start(bf16[512,256]{1,0:T(8,128)(2,1)S(1)} %get-tuple-element.65.refs_0_), channel_id=1, source_target_pairs={{0,1},{1,2},{2,3},{3,0},{4,5},{5,6},{6,7},{7,4},{8,9},{9,10},{10,1... | collective-permute-start | bytes 786440 | tf_op jit(solution)/shard_map/ppermute | solution.py:364
  59.1 30.2 %collective-permute-start.7 = (bf16[512,256]{1,0:T(8,128)(2,1)S(1)}, bf16[512,256]{1,0:T(8,128)(2,1)S(1)}, u32[]{:S(2)}, u32[]{:S(2)}) collective-permute-start(bf16[512,256]{1,0:T(8,128)(2,1)S(1)} %get-tuple-element.65.refs_0_), channel_id=1, source_target_pairs={{0,2},{1,3},{2,0},{3,1},{4,6},{5,7},{6,4},{7,5},{8,10},{9,11},{10,... | collective-permute-start | bytes 786440 | tf_op jit(solution)/shard_map/ppermute | solution.py:364
  61.8 27.6 %collective-permute-start.8 = (bf16[512,256]{1,0:T(8,128)(2,1)S(1)}, bf16[512,256]{1,0:T(8,128)(2,1)S(1)}, u32[]{:S(2)}, u32[]{:S(2)}) collective-permute-start(bf16[512,256]{1,0:T(8,128)(2,1)S(1)} %get-tuple-element.65.refs_0_), channel_id=1, source_target_pairs={{0,3},{1,0},{2,1},{3,2},{4,7},{5,4},{6,5},{7,6},{8,11},{9,8},{10,9... | collective-permute-start | bytes 786440 | tf_op jit(solution)/shard_map/ppermute | solution.py:364
  86.2 7.6 %collective-permute-start.9 = (bf16[512,256]{1,0:T(8,128)(2,1)S(1)}, bf16[512,256]{1,0:T(8,128)(2,1)S(1)}, u32[]{:S(2)}, u32[]{:S(2)}) collective-permute-start(bf16[512,256]{1,0:T(8,128)(2,1)S(1)} %get-tuple-element.69.refs_4_), channel_id=1, source_target_pairs={{0,4},{1,5},{2,6},{3,7},{4,8},{5,9},{6,10},{7,11},{8,12},{9,13},{1... | collective-permute-start | bytes 786440 | tf_op jit(solution)/shard_map/ppermute | solution.py:364
  109.0 29.4 %all-to-all-start = ((bf16[16,528,128]{2,1,0:T(8,128)(2,1)}), bf16[16,528,128]{2,1,0:T(8,128)(2,1)S(1)}, u32[]{:S(2)}, u32[]{:S(2)}) async-start(bf16[16,528,128]{2,1,0:T(8,128)(2,1)} %attend.2), calls=%async_computation | async-start | bytes 4325376 | tf_op jit(solution)/shard_map/all_to_all | solution.py:346
  121.5 12.8 %collective-permute-start.19 = (bf16[128,512]{1,0:T(8,128)(2,1)S(1)}, bf16[128,512]{1,0:T(8,128)(2,1)S(1)}, u32[]{:S(2)}, u32[]{:S(2)}) collective-permute-start(bf16[128,512]{1,0:T(8,128)(2,1)S(1)} %get-tuple-element.86), channel_id=1, source_target_pairs={{0,32},{16,48},{32,64},{48,80},{64,96},{80,112},{96,0},{112,16},{1... | collective-permute-start | bytes 393224 | tf_op jit(solution)/shard_map/ppermute | solution.py:355
  126.7 9.8 %collective-permute-start.20 = (bf16[128,512]{1,0:T(8,128)(2,1)S(1)}, bf16[128,512]{1,0:T(8,128)(2,1)S(1)}, u32[]{:S(2)}, u32[]{:S(2)}) collective-permute-start(bf16[128,512]{1,0:T(8,128)(2,1)S(1)} %get-tuple-element.87), channel_id=1, source_target_pairs={{0,96},{16,112},{32,0},{48,16},{64,32},{80,48},{96,64},{112,80},{1... | collective-permute-start | bytes 393224 | tf_op jit(solution)/shard_map/ppermute | solution.py:355
  130.6 7.7 %collective-permute-start.21 = (bf16[128,512]{1,0:T(8,128)(2,1)S(1)}, bf16[128,512]{1,0:T(8,128)(2,1)S(1)}, u32[]{:S(2)}, u32[]{:S(2)}) collective-permute-start(bf16[128,512]{1,0:T(8,128)(2,1)S(1)} %get-tuple-element.88), channel_id=1, source_target_pairs={{0,64},{16,80},{32,96},{48,112},{64,0},{80,16},{96,32},{112,48},{1... | collective-permute-start | bytes 393224 | tf_op jit(solution)/shard_map/ppermute | solution.py:355
  143.7 15.4 %collective-permute-start.23 = (bf16[128,512]{1,0:T(8,128)(2,1)S(1)}, bf16[128,512]{1,0:T(8,128)(2,1)S(1)}, u32[]{:S(2)}, u32[]{:S(2)}) collective-permute-start(bf16[128,512]{1,0:T(8,128)(2,1)S(1)} %get-tuple-element.94), channel_id=1, source_target_pairs={{0,32},{16,48},{32,64},{48,80},{64,96},{80,112},{96,0},{112,16},{1... | collective-permute-start | bytes 393224 | tf_op jit(solution)/shard_map/ppermute | solution.py:355
  155.3 6.8 %collective-permute-start.25 = (bf16[128,512]{1,0:T(8,128)(2,1)S(1)}, bf16[128,512]{1,0:T(8,128)(2,1)S(1)}, u32[]{:S(2)}, u32[]{:S(2)}) collective-permute-start(bf16[128,512]{1,0:T(8,128)(2,1)S(1)} %get-tuple-element.96), channel_id=1, source_target_pairs={{0,64},{16,80},{32,96},{48,112},{64,0},{80,16},{96,32},{112,48},{1... | collective-permute-start | bytes 393224 | tf_op jit(solution)/shard_map/ppermute | solution.py:355
  (6 other events, 18.8 us)

commit v4 on v2

--- a/solution.py
+++ b/solution.py
@@ -63,8 +63,7 @@
     dx = (me // side - owner // side) % side
     dy = (me % side - owner % side) % side
     head = jnp.arange(heads, dtype=jnp.int32)[:, None]
-    near = jnp.where(head < heads // 2, dy * side + dx, dx * side + dy)
-    position = jnp.where(chunk == 0, near, owner)
+    position = jnp.where(head < heads // 2, dy * side + dx, dx * side + dy)
     codes = (((chunk * 16 + head) * 256 + owner) * 256 + position) * 256 + tile
     smem = pl.BlockSpec(memory_space=pltpu.SMEM)
     return pl.pallas_call(
@@ -84,17 +83,16 @@
     blocks = 1 + max(i for pieces in sources for i, _ in pieces)
     q_hbm = refs[:blocks]
     k_hbm, v_hbm, out_ref, qs, ks, vs, acc, top, den, stats, sems = refs[blocks:]
-    heads, _, width = qs.shape
-    owners = qs.shape[1] // BLOCK
+    heads, owners, _, width = qs.shape
     scale = width**-0.5 * math.log2(math.e)
 
     def copies(h):
         moves = [(k_hbm.at[:, h * width : (h + 1) * width], ks.at[h])]
         moves.append((v_hbm.at[:, h * width : (h + 1) * width], vs.at[h]))
         for n, (i, lane) in enumerate(sources[h]):
-            rows = q_hbm[i].shape[0]
-            src = q_hbm[i].at[:, lane * width : (lane + 1) * width]
-            moves.append((src, qs.at[h, n * rows : (n + 1) * rows]))
+            blocks = q_hbm[i].shape[0]
+            src = q_hbm[i].at[:, chunk, :, lane * width : (lane + 1) * width]
+            moves.append((src, qs.at[h, n * blocks : (n + 1) * blocks]))
         return [
             pltpu.make_async_copy(src, dst, sems.at[h, i]) for i, (src, dst) in enumerate(moves)
         ]
@@ -135,7 +133,7 @@
         scores = [
             lax.dot_general(
                 ks[head, rows(tile), :],
-                qs[head, rows(position), :],
+                qs[head, position],
                 (((1,), (1,)), ((), ())),
                 preferred_element_type=F32,
             )
@@ -201,8 +199,7 @@
 def attend(chunk, entries, starts, queries, sources, keys, values):
     heads = len(sources)
     width = keys.shape[1] // heads
-    count = sum(queries[i].shape[0] for i, _ in sources[0])
-    owners = count // BLOCK
+    owners = sum(queries[i].shape[0] for i, _ in sources[0])
     smem = pl.BlockSpec(memory_space=pltpu.SMEM)
     hbm = pl.BlockSpec(memory_space=pl.ANY)
     lines = -(-(heads * owners + 1) // 8) * 8
@@ -211,7 +208,7 @@
         out_shape=jax.ShapeDtypeStruct((owners, heads * width + STAT_ROWS, BLOCK), BF16),
         in_specs=[smem, smem] + [hbm] * (len(queries) + 2),
         scratch_shapes=[
-            pltpu.VMEM((heads, count, width), BF16),
+            pltpu.VMEM((heads, owners, BLOCK, width), BF16),
             pltpu.VMEM((heads, keys.shape[0], width), BF16),
             pltpu.VMEM((heads, values.shape[0], width), BF16),
             pltpu.VMEM((heads * owners + 1, width, BLOCK), F32),
@@ -220,7 +217,7 @@
             pltpu.VMEM((3 * heads, owners, BLOCK), F32),
             pltpu.SemaphoreType.DMA((heads, 2 + max(len(p) for p in sources))),
         ],
-        compiler_params=pltpu.CompilerParams(vmem_limit_bytes=40 * 1024 * 1024),
+        compiler_params=pltpu.CompilerParams(vmem_limit_bytes=50 * 1024 * 1024),
         name="attend",
     )(entries, starts, *queries, in_hbm(keys), in_hbm(values))
 
@@ -278,7 +275,7 @@
                 pltpu.SemaphoreType.DMA((zs, 2)),
             ],
         ),
-        compiler_params=pltpu.CompilerParams(vmem_limit_bytes=24 * 1024 * 1024),
+        compiler_params=pltpu.CompilerParams(vmem_limit_bytes=14 * 1024 * 1024),
         name="project",
     )(core, parts, in_hbm(weight))
 
@@ -333,9 +330,6 @@
             total = total + lax.ppermute(piece, "heads", pairs).astype(F32)
         return total.astype(BF16)
 
-    def rows(c):
-        return queries[c * BLOCK : (c + 1) * BLOCK]
-
     def along(x, axis):
         def pairs(d):
             there = lambda i, j: ((i + d) % side, j) if axis == 0 else (i, (j + d) % side)
@@ -345,28 +339,25 @@
         got = {d: lax.ppermute(x, "keys", pairs(d)) for d in Z_STEPS}
         return [x] + [got[d] for d in range(1, side)]
 
-    near = rows(0)
-    middle = near.shape[1] // 2
-    left, right = near[:, :middle], near[:, middle:]
+    middle = queries.shape[1] // 2
+    left, right = queries[:, :middle], queries[:, middle:]
     left, right = lax.optimization_barrier((left, right))
-    halves = along(left, 0) + along(right, 1)
-    halves = lax.optimization_barrier(halves)
+    halves = lax.optimization_barrier(along(left, 0) + along(right, 1))
+
     left, right = jnp.concatenate(halves[:side]), jnp.concatenate(halves[side:])
     left, right = lax.optimization_barrier((left, right))
-    direct = lax.optimization_barrier(along(left, 1) + along(right, 0))
+    everything = lax.optimization_barrier(along(left, 1) + along(right, 0))
+    everything = [x.reshape(side, owned, BLOCK, middle) for x in everything]
     lower = [[(i, h) for i in range(side)] for h in range(heads // 2)]
     upper = [[(side + i, h) for i in range(side)] for h in range(heads // 2)]
-    whole = [[(0, h)] for h in range(heads)]
 
     slot = jnp.reshape(lax.axis_index("keys"), (1,)).astype(jnp.int32)
     entries, starts = plan(slot, block_ids, block_counts, tiles, owned, side)
     outs = []
     for c in range(owned):
-        if c == 0:
-            source, lanes = direct, lower + upper
-        else:
-            source, lanes = [in_hbm(lax.all_gather(rows(c), "keys", axis=0, tiled=True))], whole
-        parts = attend(c, entries, starts, source, lanes, key_states, value_states)
+        parts = attend(
+            c, entries, starts, everything, lower + upper, key_states, value_states
+        )
         got = exchange(parts)
         if outs:
             got, outs[-1] = lax.optimization_barrier((got, outs[-1]))

time: 150 us -> 156 us (1.040)
  waiting for transfers between devices: 48.8 us -> 69.4 us
  between operations: 13.6 us -> 0.23 us
  starting transfers between devices: 40.4 us -> 38 us
  local copies, waits for them, and re-layouts: 6.14 us -> 8.23 us
    ppermute x12, waiting for transfers between devices: 4.82 us -> 24.5 us  [along(): got = {d: lax.ppermute(x, 'keys', pairs(d)) for d in Z_STEPS}]
    ppermute x12, starting transfers between devices: 22.4 us -> 17.6 us  [along(): got = {d: lax.ppermute(x, 'keys', pairs(d)) for d in Z_STEPS}]
    all_to_all x2, starting transfers between devices: 7.72 us -> 12.3 us  [exchange(): lax.all_to_all(parts, 'keys', split_axis=0, concat_axis=0, tiled=True)]
    unnamed x5 -> x25, local copies, waits for them, and re-layouts: 3.69 us -> 7.22 us
    ppermute x6, starting transfers between devices: 10.1 us -> 7.92 us  [finish(): total = total + lax.ppermute(piece, 'heads', pairs).astype(F32)]
  transfers between devices with their start and end apart: 23 -> 22, of which waited for: 15 -> 20; matrix products, arithmetic and copies ran while one was open for 2% -> 0% of each run, Pallas kernels for 23% -> 14%
where the time goes in v4:
time: 156 us; the launch traced here: 153 us
  waiting for transfers between devices  69.4 us (44%)
  starting transfers between devices  38 us (24%)
  Pallas kernels  36.4 us (23%)
  local copies, waits for them, and re-layouts  8.23 us (5%)
    all_to_all x2, waiting for transfers between devices, exchange(): lax.all_to_all(parts, 'keys', split_axis=0, concat_axis=0, tiled=True)  29.3 us
    pallas_call x2, Pallas kernels, attend(): pl.pallas_call(functools.partial(attend_kernel, chunk, sources), out_shap...  24.7 us
    ppermute x12, waiting for transfers between devices, along(): got = {d: lax.ppermute(x, 'keys', pairs(d)) for d in Z_STEPS}  24.5 us
    ppermute x12, starting transfers between devices, along(): got = {d: lax.ppermute(x, 'keys', pairs(d)) for d in Z_STEPS}  17.6 us
    all_to_all x2, starting transfers between devices, exchange(): lax.all_to_all(parts, 'keys', split_axis=0, concat_axis=0, tiled=True)  12.3 us
    ppermute x6, waiting for transfers between devices, finish(): total = total + lax.ppermute(piece, 'heads', pairs).astype(F32)  11.6 us
    ppermute x6, starting transfers between devices, finish(): total = total + lax.ppermute(piece, 'heads', pairs).astype(F32)  7.92 us
    unnamed x25, local copies, waits for them, and re-layouts  7.22 us
  transfers between devices with their start and end apart: 22, of which 20 were waited for; matrix products, arithmetic and copies ran while one was open for 0% of the time, Pallas kernels for 14%

profile of v4, /device:TPU:0, one launch (start us, length us, event | category | flops | bytes accessed | tf_op | source)
XLA Modules:
  0.0 153.4 jit_solution(1223395460685387443)
XLA Ops:
  1.0 2.9 %collective-permute-start.2 = (bf16[256,256]{1,0:T(8,128)(2,1)S(1)}, bf16[256,256]{1,0:T(8,128)(2,1)S(1)}, u32[]{:S(2)}, u32[]{:S(2)}) collective-permute-start(bf16[256,256]{1,0:T(8,128)(2,1)S(1)} %get-tuple-element.45), channel_id=1, source_target_pairs={{0,12},{1,13},{2,14},{3,15},{4,0},{5,1},{6,2},{7,3},{8,4},{9,5},{1... | collective-permute-start | bytes 393224 | tf_op jit(solution)/shard_map/ppermute | solution.py:339
  5.6 3.0 %collective-permute-start.5 = (bf16[256,256]{1,0:T(8,128)(2,1)S(1)}, bf16[256,256]{1,0:T(8,128)(2,1)S(1)}, u32[]{:S(2)}, u32[]{:S(2)}) collective-permute-start(bf16[256,256]{1,0:T(8,128)(2,1)S(1)} %get-tuple-element.49), channel_id=1, source_target_pairs={{0,3},{1,0},{2,1},{3,2},{4,7},{5,4},{6,5},{7,6},{8,11},{9,8},{10,9... | collective-permute-start | bytes 393224 | tf_op jit(solution)/shard_map/ppermute | solution.py:339
  13.4 2.3 %collective-permute-done.4 = bf16[256,256]{1,0:T(8,128)(2,1)S(1)} collective-permute-done((bf16[256,256]{1,0:T(8,128)(2,1)S(1)}, bf16[256,256]{1,0:T(8,128)(2,1)S(1)}, u32[]{:S(2)}, u32[]{:S(2)}) %collective-permute-start.4) | collective-permute-done | bytes 131104 | tf_op jit(solution)/shard_map/ppermute | solution.py:339
  19.3 3.7 %collective-permute-start.11 = (bf16[1024,256]{1,0:T(8,128)(2,1)S(1)}, bf16[1024,256]{1,0:T(8,128)(2,1)}, u32[]{:S(2)}, u32[]{:S(2)}) collective-permute-start(bf16[1024,256]{1,0:T(8,128)(2,1)S(1)} %get-tuple-element.59), channel_id=1, source_target_pairs={{0,12},{1,13},{2,14},{3,15},{4,0},{5,1},{6,2},{7,3},{8,4},{9,5},{1... | collective-permute-start | bytes 1572872 | tf_op jit(solution)/shard_map/ppermute | solution.py:339
  23.1 8.9 %collective-permute-done.8 = bf16[1024,256]{1,0:T(8,128)(2,1)S(1)} collective-permute-done((bf16[1024,256]{1,0:T(8,128)(2,1)S(1)}, bf16[1024,256]{1,0:T(8,128)(2,1)S(1)}, u32[]{:S(2)}, u32[]{:S(2)}) %collective-permute-start.8) | collective-permute-done | bytes 524320 | tf_op jit(solution)/shard_map/ppermute | solution.py:339
  34.0 4.4 %plan.1 = (s32[2,776]{1,0:T(2,128)S(1)}, s32[2,5]{1,0:T(2,128)S(1)}) custom-call(s32[4,192]{1,0:T(4,128)S(1)} %fusion.7.codes, s32[4,1]{1,0:T(4,128)S(1)} %copy.7.counts), custom_call_target="tpu_custom_call" | custom-call | tf_op jit(solution)/shard_map/plan/pallas_call | solution.py:69
  38.4 4.3 %collective-permute-done.6 = bf16[1024,256]{1,0:T(8,128)(2,1)S(1)} collective-permute-done((bf16[1024,256]{1,0:T(8,128)(2,1)S(1)}, bf16[1024,256]{1,0:T(8,128)(2,1)S(1)}, u32[]{:S(2)}, u32[]{:S(2)}) %collective-permute-start.6) | collective-permute-done | bytes 524320 | tf_op jit(solution)/shard_map/ppermute | solution.py:339
  44.0 3.8 %collective-permute-done.9 = bf16[1024,256]{1,0:T(8,128)(2,1)} collective-permute-done((bf16[1024,256]{1,0:T(8,128)(2,1)S(1)}, bf16[1024,256]{1,0:T(8,128)(2,1)}, u32[]{:S(2)}, u32[]{:S(2)}) %collective-permute-start.9) | collective-permute-done | bytes 524320 | tf_op jit(solution)/shard_map/ppermute | solution.py:339
  47.8 12.4 %attend.3 = bf16[16,528,128]{2,1,0:T(8,128)(2,1)} custom-call(s32[2,776]{1,0:T(2,128)S(1)} %get-tuple-element.41.entries, s32[2,5]{1,0:T(2,128)S(1)} %get-tuple-element.42.starts, bf16[4,2,128,256]{3,2,1,0:T(8,128)(2,1)S(1)} %bitcast.13, bf16[4,2,128,256]{3,2,1,0:T(8,128)(2,1)S(1)} %bitcast.21, bf16[4,2,128,256]{3,2,1,0:T(8,128)(2,1)S(1)} %bitcast.19, ...), custom_call_target="tpu_custom_call" | custom-call | tf_op jit(solution)/shard_map/attend/pallas_call | solution.py:206
  60.3 5.2 %all-to-all-start.1 = ((bf16[16,528,128]{2,1,0:T(8,128)(2,1)}), bf16[16,528,128]{2,1,0:T(8,128)(2,1)S(1)}, u32[]{:S(2)}, u32[]{:S(2)}) async-start(bf16[16,528,128]{2,1,0:T(8,128)(2,1)} %attend.3), calls=%async_computation.1 | async-start | bytes 4325376 | tf_op jit(solution)/shard_map/all_to_all | solution.py:321
  69.6 12.3 %attend.2 = bf16[16,528,128]{2,1,0:T(8,128)(2,1)} custom-call(s32[2,776]{1,0:T(2,128)S(1)} %get-tuple-element.41.entries, s32[2,5]{1,0:T(2,128)S(1)} %get-tuple-element.42.starts, bf16[4,2,128,256]{3,2,1,0:T(8,128)(2,1)S(1)} %bitcast.14, bf16[4,2,128,256]{3,2,1,0:T(8,128)(2,1)S(1)} %bitcast.22, bf16[4,2,128,256]{3,2,1,0:T(8,128)(2,1)S(1)} %bitcast.20, ...), custom_call_target="tpu_custom_call" | custom-call | tf_op jit(solution)/shard_map/attend/pallas_call | solution.py:206
  81.9 15.2 %all-to-all-done.1.in_ref = bf16[16,528,128]{2,1,0:T(8,128)(2,1)S(1)} async-done(((bf16[16,528,128]{2,1,0:T(8,128)(2,1)}), bf16[16,528,128]{2,1,0:T(8,128)(2,1)S(1)}, u32[]{:S(2)}, u32[]{:S(2)}) %all-to-all-start.1) | async-done | bytes 2162720 | tf_op jit(solution)/shard_map/all_to_all | solution.py:321
  98.5 7.1 %all-to-all-start = ((bf16[16,528,128]{2,1,0:T(8,128)(2,1)}), bf16[16,528,128]{2,1,0:T(8,128)(2,1)S(1)}, u32[]{:S(2)}, u32[]{:S(2)}) async-start(bf16[16,528,128]{2,1,0:T(8,128)(2,1)} %attend.2), calls=%async_computation | async-start | bytes 4325376 | tf_op jit(solution)/shard_map/all_to_all | solution.py:321
  107.2 4.0 %project.2 = (bf16[4,128,512]{2,1,0:T(8,128)(2,1)S(1)}, bf16[4,128,512]{2,1,0:T(8,128)(2,1)}) custom-call(s32[1]{0:T(128)} %bitcast.12.core, bf16[16,528,128]{2,1,0:T(8,128)(2,1)S(1)} %copy-done.1, bf16[512,4096]{1,0:T(8,128)(2,1)} %weight.3), custom_call_target="tpu_custom_call" | custom-call | tf_op jit(solution)/shard_map/project/pallas_call | solution.py:261
  111.3 2.1 %collective-permute-done.12.theirs = bf16[4,128,512]{2,1,0:T(8,128)(2,1)S(1)} collective-permute-done((bf16[4,128,512]{2,1,0:T(8,128)(2,1)}, bf16[4,128,512]{2,1,0:T(8,128)(2,1)S(1)}, u32[]{:S(2)}, u32[]{:S(2)}) %collective-permute-start.12) | collective-permute-done | bytes 524320 | tf_op jit(solution)/shard_map/ppermute | solution.py:326
  113.6 3.2 %collective-permute-start.14 = (bf16[128,512]{1,0:T(8,128)(2,1)S(1)}, bf16[128,512]{1,0:T(8,128)(2,1)S(1)}, u32[]{:S(2)}, u32[]{:S(2)}) collective-permute-start(bf16[128,512]{1,0:T(8,128)(2,1)S(1)} %get-tuple-element.67), channel_id=1, source_target_pairs={{0,96},{16,112},{32,0},{48,16},{64,32},{80,48},{96,64},{112,80},{1... | collective-permute-start | bytes 393224 | tf_op jit(solution)/shard_map/ppermute | solution.py:330
  118.1 2.2 %collective-permute-done.13 = bf16[128,512]{1,0:T(8,128)(2,1)S(1)} collective-permute-done((bf16[128,512]{1,0:T(8,128)(2,1)S(1)}, bf16[128,512]{1,0:T(8,128)(2,1)S(1)}, u32[]{:S(2)}, u32[]{:S(2)}) %collective-permute-start.13) | collective-permute-done | bytes 131104 | tf_op jit(solution)/shard_map/ppermute | solution.py:330
  120.3 2.1 %collective-permute-done.14 = bf16[128,512]{1,0:T(8,128)(2,1)S(1)} collective-permute-done((bf16[128,512]{1,0:T(8,128)(2,1)S(1)}, bf16[128,512]{1,0:T(8,128)(2,1)S(1)}, u32[]{:S(2)}, u32[]{:S(2)}) %collective-permute-start.14) | collective-permute-done | bytes 131104 | tf_op jit(solution)/shard_map/ppermute | solution.py:330
  123.4 14.1 %all-to-all-done.in_ref = bf16[16,528,128]{2,1,0:T(8,128)(2,1)S(1)} async-done(((bf16[16,528,128]{2,1,0:T(8,128)(2,1)}), bf16[16,528,128]{2,1,0:T(8,128)(2,1)S(1)}, u32[]{:S(2)}, u32[]{:S(2)}) %all-to-all-start) | async-done | bytes 2162720 | tf_op jit(solution)/shard_map/all_to_all | solution.py:321
  137.5 3.2 %project.3 = (bf16[4,128,512]{2,1,0:T(8,128)(2,1)S(1)}, bf16[4,128,512]{2,1,0:T(8,128)(2,1)S(1)}) custom-call(s32[1]{0:T(128)} %bitcast.12.core, bf16[16,528,128]{2,1,0:T(8,128)(2,1)S(1)} %all-to-all-done.in_ref, bf16[512,4096]{1,0:T(8,128)(2,1)} %weight.3), custom_call_target="tpu_custom_call" | custom-call | tf_op jit(solution)/shard_map/project/pallas_call | solution.py:261
  140.8 1.9 %collective-permute-done.16.theirs = bf16[4,128,512]{2,1,0:T(8,128)(2,1)S(1)} collective-permute-done((bf16[4,128,512]{2,1,0:T(8,128)(2,1)S(1)}, bf16[4,128,512]{2,1,0:T(8,128)(2,1)S(1)}, u32[]{:S(2)}, u32[]{:S(2)}) %collective-permute-start.16) | collective-permute-done | bytes 524320 | tf_op jit(solution)/shard_map/ppermute | solution.py:326
  142.9 3.2 %collective-permute-start.18 = (bf16[128,512]{1,0:T(8,128)(2,1)S(1)}, bf16[128,512]{1,0:T(8,128)(2,1)S(1)}, u32[]{:S(2)}, u32[]{:S(2)}) collective-permute-start(bf16[128,512]{1,0:T(8,128)(2,1)S(1)} %get-tuple-element.75), channel_id=1, source_target_pairs={{0,96},{16,112},{32,0},{48,16},{64,32},{80,48},{96,64},{112,80},{1... | collective-permute-start | bytes 393224 | tf_op jit(solution)/shard_map/ppermute | solution.py:330
  146.1 3.5 %collective-permute-done.17 = bf16[128,512]{1,0:T(8,128)(2,1)S(1)} collective-permute-done((bf16[128,512]{1,0:T(8,128)(2,1)S(1)}, bf16[128,512]{1,0:T(8,128)(2,1)S(1)}, u32[]{:S(2)}, u32[]{:S(2)}) %collective-permute-start.17) | collective-permute-done | bytes 131104 | tf_op jit(solution)/shard_map/ppermute | solution.py:330
  149.6 2.1 %collective-permute-done.18 = bf16[128,512]{1,0:T(8,128)(2,1)S(1)} collective-permute-done((bf16[128,512]{1,0:T(8,128)(2,1)S(1)}, bf16[128,512]{1,0:T(8,128)(2,1)S(1)}, u32[]{:S(2)}, u32[]{:S(2)}) %collective-permute-start.18) | collective-permute-done | bytes 131104 | tf_op jit(solution)/shard_map/ppermute | solution.py:330
  (59 shorter events, 26.0 us)
Async XLA Ops:
  0.0 33.9 %copy-start.11 = (s32[4,1]{0,1:T(1,128)S(1)}, s32[4,1]{0,1:T(1,128)}, u32[]{:S(2)}) copy-start(s32[4,1]{0,1:T(1,128)} %param.10) | copy-start | bytes 52
  0.0 34.0 %copy-start.10 = (s32[4,192]{1,0:T(4,128)S(1)}, s32[4,192]{1,0:T(4,128)}, u32[]{:S(2)}) copy-start(s32[4,192]{1,0:T(4,128)} %param.9) | copy-start | bytes 9220
  1.0 8.5 %collective-permute-start.2 = (bf16[256,256]{1,0:T(8,128)(2,1)S(1)}, bf16[256,256]{1,0:T(8,128)(2,1)S(1)}, u32[]{:S(2)}, u32[]{:S(2)}) collective-permute-start(bf16[256,256]{1,0:T(8,128)(2,1)S(1)} %get-tuple-element.45), channel_id=1, source_target_pairs={{0,12},{1,13},{2,14},{3,15},{4,0},{5,1},{6,2},{7,3},{8,4},{9,5},{1... | collective-permute-start | bytes 393224 | tf_op jit(solution)/shard_map/ppermute | solution.py:339
  3.9 7.9 %collective-permute-start.1 = (bf16[256,256]{1,0:T(8,128)(2,1)S(1)}, bf16[256,256]{1,0:T(8,128)(2,1)S(1)}, u32[]{:S(2)}, u32[]{:S(2)}) collective-permute-start(bf16[256,256]{1,0:T(8,128)(2,1)S(1)} %get-tuple-element.45), channel_id=1, source_target_pairs={{0,8},{1,9},{2,10},{3,11},{4,12},{5,13},{6,14},{7,15},{8,0},{9,1},... | collective-permute-start | bytes 393224 | tf_op jit(solution)/shard_map/ppermute | solution.py:339
  4.7 8.5 %collective-permute-start = (bf16[256,256]{1,0:T(8,128)(2,1)S(1)}, bf16[256,256]{1,0:T(8,128)(2,1)S(1)}, u32[]{:S(2)}, u32[]{:S(2)}) collective-permute-start(bf16[256,256]{1,0:T(8,128)(2,1)S(1)} %get-tuple-element.45), channel_id=1, source_target_pairs={{0,4},{1,5},{2,6},{3,7},{4,8},{5,9},{6,10},{7,11},{8,12},{9,13},{1... | collective-permute-start | bytes 393224 | tf_op jit(solution)/shard_map/ppermute | solution.py:339
  5.6 7.8 %collective-permute-start.5 = (bf16[256,256]{1,0:T(8,128)(2,1)S(1)}, bf16[256,256]{1,0:T(8,128)(2,1)S(1)}, u32[]{:S(2)}, u32[]{:S(2)}) collective-permute-start(bf16[256,256]{1,0:T(8,128)(2,1)S(1)} %get-tuple-element.49), channel_id=1, source_target_pairs={{0,3},{1,0},{2,1},{3,2},{4,7},{5,4},{6,5},{7,6},{8,11},{9,8},{10,9... | collective-permute-start | bytes 393224 | tf_op jit(solution)/shard_map/ppermute | solution.py:339
  8.6 7.1 %collective-permute-start.4 = (bf16[256,256]{1,0:T(8,128)(2,1)S(1)}, bf16[256,256]{1,0:T(8,128)(2,1)S(1)}, u32[]{:S(2)}, u32[]{:S(2)}) collective-permute-start(bf16[256,256]{1,0:T(8,128)(2,1)S(1)} %get-tuple-element.49), channel_id=1, source_target_pairs={{0,2},{1,3},{2,0},{3,1},{4,6},{5,7},{6,4},{7,5},{8,10},{9,11},{10,... | collective-permute-start | bytes 393224 | tf_op jit(solution)/shard_map/ppermute | solution.py:339
  9.5 7.6 %collective-permute-start.3 = (bf16[256,256]{1,0:T(8,128)(2,1)S(1)}, bf16[256,256]{1,0:T(8,128)(2,1)S(1)}, u32[]{:S(2)}, u32[]{:S(2)}) collective-permute-start(bf16[256,256]{1,0:T(8,128)(2,1)S(1)} %get-tuple-element.49), channel_id=1, source_target_pairs={{0,1},{1,2},{2,3},{3,0},{4,5},{5,6},{6,7},{7,4},{8,9},{9,10},{10,1... | collective-permute-start | bytes 393224 | tf_op jit(solution)/shard_map/ppermute | solution.py:339
  17.1 14.9 %collective-permute-start.8 = (bf16[1024,256]{1,0:T(8,128)(2,1)S(1)}, bf16[1024,256]{1,0:T(8,128)(2,1)S(1)}, u32[]{:S(2)}, u32[]{:S(2)}) collective-permute-start(bf16[1024,256]{1,0:T(8,128)(2,1)S(1)} %get-tuple-element.55), channel_id=1, source_target_pairs={{0,3},{1,0},{2,1},{3,2},{4,7},{5,4},{6,5},{7,6},{8,11},{9,8},{10,9... | collective-permute-start | bytes 1572872 | tf_op jit(solution)/shard_map/ppermute | solution.py:339
  17.8 20.7 %collective-permute-start.7 = (bf16[1024,256]{1,0:T(8,128)(2,1)S(1)}, bf16[1024,256]{1,0:T(8,128)(2,1)S(1)}, u32[]{:S(2)}, u32[]{:S(2)}) collective-permute-start(bf16[1024,256]{1,0:T(8,128)(2,1)S(1)} %get-tuple-element.55), channel_id=1, source_target_pairs={{0,2},{1,3},{2,0},{3,1},{4,6},{5,7},{6,4},{7,5},{8,10},{9,11},{10,... | collective-permute-start | bytes 1572872 | tf_op jit(solution)/shard_map/ppermute | solution.py:339
  18.4 24.3 %collective-permute-start.6 = (bf16[1024,256]{1,0:T(8,128)(2,1)S(1)}, bf16[1024,256]{1,0:T(8,128)(2,1)S(1)}, u32[]{:S(2)}, u32[]{:S(2)}) collective-permute-start(bf16[1024,256]{1,0:T(8,128)(2,1)S(1)} %get-tuple-element.55), channel_id=1, source_target_pairs={{0,1},{1,2},{2,3},{3,0},{4,5},{5,6},{6,7},{7,4},{8,9},{9,10},{10,1... | collective-permute-start | bytes 1572872 | tf_op jit(solution)/shard_map/ppermute | solution.py:339
  19.3 24.7 %collective-permute-start.11 = (bf16[1024,256]{1,0:T(8,128)(2,1)S(1)}, bf16[1024,256]{1,0:T(8,128)(2,1)}, u32[]{:S(2)}, u32[]{:S(2)}) collective-permute-start(bf16[1024,256]{1,0:T(8,128)(2,1)S(1)} %get-tuple-element.59), channel_id=1, source_target_pairs={{0,12},{1,13},{2,14},{3,15},{4,0},{5,1},{6,2},{7,3},{8,4},{9,5},{1... | collective-permute-start | bytes 1572872 | tf_op jit(solution)/shard_map/ppermute | solution.py:339
  22.9 21.1 %collective-permute-start.10 = (bf16[1024,256]{1,0:T(8,128)(2,1)S(1)}, bf16[1024,256]{1,0:T(8,128)(2,1)S(1)}, u32[]{:S(2)}, u32[]{:S(2)}) collective-permute-start(bf16[1024,256]{1,0:T(8,128)(2,1)S(1)} %get-tuple-element.59), channel_id=1, source_target_pairs={{0,8},{1,9},{2,10},{3,11},{4,12},{5,13},{6,14},{7,15},{8,0},{9,1},... | collective-permute-start | bytes 1572872 | tf_op jit(solution)/shard_map/ppermute | solution.py:339
  32.1 15.7 %collective-permute-start.9 = (bf16[1024,256]{1,0:T(8,128)(2,1)S(1)}, bf16[1024,256]{1,0:T(8,128)(2,1)}, u32[]{:S(2)}, u32[]{:S(2)}) collective-permute-start(bf16[1024,256]{1,0:T(8,128)(2,1)S(1)} %get-tuple-element.59), channel_id=1, source_target_pairs={{0,4},{1,5},{2,6},{3,7},{4,8},{5,9},{6,10},{7,11},{8,12},{9,13},{1... | collective-permute-start | bytes 1572872 | tf_op jit(solution)/shard_map/ppermute | solution.py:339
  60.3 36.9 %all-to-all-start.1 = ((bf16[16,528,128]{2,1,0:T(8,128)(2,1)}), bf16[16,528,128]{2,1,0:T(8,128)(2,1)S(1)}, u32[]{:S(2)}, u32[]{:S(2)}) async-start(bf16[16,528,128]{2,1,0:T(8,128)(2,1)} %attend.3), calls=%async_computation.1 | async-start | bytes 4325376 | tf_op jit(solution)/shard_map/all_to_all | solution.py:321
  98.5 39.0 %all-to-all-start = ((bf16[16,528,128]{2,1,0:T(8,128)(2,1)}), bf16[16,528,128]{2,1,0:T(8,128)(2,1)S(1)}, u32[]{:S(2)}, u32[]{:S(2)}) async-start(bf16[16,528,128]{2,1,0:T(8,128)(2,1)} %attend.2), calls=%async_computation | async-start | bytes 4325376 | tf_op jit(solution)/shard_map/all_to_all | solution.py:321
  111.2 2.2 %collective-permute-start.12 = (bf16[4,128,512]{2,1,0:T(8,128)(2,1)}, bf16[4,128,512]{2,1,0:T(8,128)(2,1)S(1)}, u32[]{:S(2)}, u32[]{:S(2)}) collective-permute-start(bf16[4,128,512]{2,1,0:T(8,128)(2,1)} %get-tuple-element.64), channel_id=1, source_target_pairs={{0,16},{16,0},{32,48},{48,32},{64,80},{80,64},{96,112},{112,96},{1... | collective-permute-start | bytes 1572872 | tf_op jit(solution)/shard_map/ppermute | solution.py:326
  113.5 6.8 %collective-permute-start.13 = (bf16[128,512]{1,0:T(8,128)(2,1)S(1)}, bf16[128,512]{1,0:T(8,128)(2,1)S(1)}, u32[]{:S(2)}, u32[]{:S(2)}) collective-permute-start(bf16[128,512]{1,0:T(8,128)(2,1)S(1)} %get-tuple-element.66), channel_id=1, source_target_pairs={{0,32},{16,48},{32,64},{48,80},{64,96},{80,112},{96,0},{112,16},{1... | collective-permute-start | bytes 393224 | tf_op jit(solution)/shard_map/ppermute | solution.py:330
  113.6 8.8 %collective-permute-start.14 = (bf16[128,512]{1,0:T(8,128)(2,1)S(1)}, bf16[128,512]{1,0:T(8,128)(2,1)S(1)}, u32[]{:S(2)}, u32[]{:S(2)}) collective-permute-start(bf16[128,512]{1,0:T(8,128)(2,1)S(1)} %get-tuple-element.67), channel_id=1, source_target_pairs={{0,96},{16,112},{32,0},{48,16},{64,32},{80,48},{96,64},{112,80},{1... | collective-permute-start | bytes 393224 | tf_op jit(solution)/shard_map/ppermute | solution.py:330
  116.8 6.5 %collective-permute-start.15 = (bf16[128,512]{1,0:T(8,128)(2,1)S(1)}, bf16[128,512]{1,0:T(8,128)(2,1)S(1)}, u32[]{:S(2)}, u32[]{:S(2)}) collective-permute-start(bf16[128,512]{1,0:T(8,128)(2,1)S(1)} %get-tuple-element.68), channel_id=1, source_target_pairs={{0,64},{16,80},{32,96},{48,112},{64,0},{80,16},{96,32},{112,48},{1... | collective-permute-start | bytes 393224 | tf_op jit(solution)/shard_map/ppermute | solution.py:330
  140.7 2.0 %collective-permute-start.16 = (bf16[4,128,512]{2,1,0:T(8,128)(2,1)S(1)}, bf16[4,128,512]{2,1,0:T(8,128)(2,1)S(1)}, u32[]{:S(2)}, u32[]{:S(2)}) collective-permute-start(bf16[4,128,512]{2,1,0:T(8,128)(2,1)S(1)} %get-tuple-element.72), channel_id=1, source_target_pairs={{0,16},{16,0},{32,48},{48,32},{64,80},{80,64},{96,112},{112,96},{1... | collective-permute-start | bytes 1572872 | tf_op jit(solution)/shard_map/ppermute | solution.py:326
  142.8 6.8 %collective-permute-start.17 = (bf16[128,512]{1,0:T(8,128)(2,1)S(1)}, bf16[128,512]{1,0:T(8,128)(2,1)S(1)}, u32[]{:S(2)}, u32[]{:S(2)}) collective-permute-start(bf16[128,512]{1,0:T(8,128)(2,1)S(1)} %get-tuple-element.74), channel_id=1, source_target_pairs={{0,32},{16,48},{32,64},{48,80},{64,96},{80,112},{96,0},{112,16},{1... | collective-permute-start | bytes 393224 | tf_op jit(solution)/shard_map/ppermute | solution.py:330
  142.9 8.8 %collective-permute-start.18 = (bf16[128,512]{1,0:T(8,128)(2,1)S(1)}, bf16[128,512]{1,0:T(8,128)(2,1)S(1)}, u32[]{:S(2)}, u32[]{:S(2)}) collective-permute-start(bf16[128,512]{1,0:T(8,128)(2,1)S(1)} %get-tuple-element.75), channel_id=1, source_target_pairs={{0,96},{16,112},{32,0},{48,16},{64,32},{80,48},{96,64},{112,80},{1... | collective-permute-start | bytes 393224 | tf_op jit(solution)/shard_map/ppermute | solution.py:330
  146.1 6.5 %collective-permute-start.19 = (bf16[128,512]{1,0:T(8,128)(2,1)S(1)}, bf16[128,512]{1,0:T(8,128)(2,1)S(1)}, u32[]{:S(2)}, u32[]{:S(2)}) collective-permute-start(bf16[128,512]{1,0:T(8,128)(2,1)S(1)} %get-tuple-element.76), channel_id=1, source_target_pairs={{0,64},{16,80},{32,96},{48,112},{64,0},{80,16},{96,32},{112,48},{1... | collective-permute-start | bytes 393224 | tf_op jit(solution)/shard_map/ppermute | solution.py:330
  (10 other events, 90.8 us)
